TPU v7x, 256 devices: a whole 4x4x8 slice. The times are simulated.
256 devices in a mesh: expert: 128 (over x, z, y), dp: 2 (over core).
Axes of the slice: x: 4, y: 4, z: 8, core: 2. Of those that a mesh axis runs over, the one named last changes fastest.
Arguments:
- pooled: bfloat16 [65536, 256], P(('expert', 'dp')), may hold values from -6 to 6
- routes: int32 [65536, 2], P(('expert', 'dp')), may hold values from 0 to 127, all different within a row; in each aligned block of 256 rows (0 to 255, 256 to 511, ...) at most 6 rows name the same one
- labels: int32 [65536, 2], P(('expert', 'dp')), may hold values from 0 to 1
- in_weight: bfloat16 [128, 4096, 256], P('expert'), may hold values from -0.375 to 0.375
- out_weight: bfloat16 [128, 4096, 256], P('expert'), may hold values from -0.09375 to 0.09375
- gate_weight: bfloat16 [128, 2, 256], replicated, may hold values from -0.375 to 0.375
- tower_weight: float32 [2, 256], replicated, may hold values from -0.375 to 0.375
- tower_bias: float32 [2], replicated, may hold values from -3 to 3
- bag_rows: int32 [131072], P(('expert', 'dp')), may hold values from 0 to 1023
- bag_sample: int32 [131072], P(('expert', 'dp')), may hold values from 0 to 255
- bag_weight: float32 [131072], P(('expert', 'dp')), may hold values from 0.5 to 2
- row_table: float32 [131072, 256], P('expert'), may hold values from -6 to 6
Outputs:
- in_grad: float32 [128, 4096, 256], P('expert', 'dp')
- out_grad: float32 [128, 4096, 256], P('expert', 'dp')
- gate_grad: float32 [128, 2, 256], P('expert')
- tower_grad: float32 [2, 256], replicated
- new_table: float32 [131072, 256], P('expert')
Inputs may be any that keep to these rules, and one draw needn't show every extreme that they name: `routes`: within each device's 256 rows no expert is named more than 6 times, a bound that some block reaches; a row's two experts differ.
All inputs are finite; a program needn't handle non-finite values.
Results may differ from a plain program's by a relative error of at most 0.0041.
Values may be sent and summed in bfloat16 or wider, within the bound.
No kernel may reach another device: no remote copies, remote signals or barrier semaphores. Data moves between devices by JAX's collectives and lax.ppermute only.
A program may use at most 128 MiB of HBM per device.

v0:
```python
import functools

import jax
import jax.numpy as jnp
from jax import lax
from jax.experimental import pallas as pl
from jax.experimental.pallas import tpu as pltpu
from jax.sharding import Mesh
from jax.sharding import PartitionSpec as P

EXPERT = ("expert_0", "expert_1", "expert_2")
EXPERT_DP = ("expert_0", "expert_1", "expert_2", "dp")

LOSS_SCALE = 32.0
STEP_SIZE = 0.25
BF = jnp.bfloat16
F32 = jnp.float32

ROWS = 2
BLOCKS = 3
PIECES = 3
SLOT_LANES = 4 * PIECES
ROW_LANES = BLOCKS * SLOT_LANES


def dot(left, right):
    return jnp.dot(left, right, preferred_element_type=F32)


def dot_last(left, right):
    return lax.dot_general(left, right, (((1,), (1,)), ((), ())), preferred_element_type=F32)


def iota(shape, dim):
    return lax.broadcasted_iota(jnp.int32, shape, dim)


def ones_where(mask):
    return jnp.where(mask, 1.0, 0.0).astype(BF)


def three_pieces(value):
    high = value.astype(BF)
    rest = value - high.astype(F32)
    middle = rest.astype(BF)
    low = (rest - middle.astype(F32)).astype(BF)
    return high, middle, low


def tower_pieces(tower):
    pieces = three_pieces(tower)
    row = iota((8, tower.shape[1]), 0)
    stacked = jnp.zeros((8, tower.shape[1]), F32)
    for p, piece in enumerate(pieces):
        for t in range(2):
            stacked = jnp.where(row == 2 * p + t, piece[t : t + 1].astype(F32), stacked)
    return stacked.astype(BF)


def silu_and_slope(pre):
    sigma = 0.5 * jnp.tanh(0.5 * pre) + 0.5
    act = pre * sigma
    return act, sigma + act * (1.0 - sigma)


def full(shape):
    return pl.BlockSpec(shape, lambda *_: (0,) * len(shape))


def call(kernel, out_shape, ins, flops, name, **more):
    return pl.pallas_call(
        kernel,
        out_shape=out_shape,
        cost_estimate=pl.CostEstimate(flops=flops, transcendentals=0, bytes_accessed=1 << 20),
        name=name,
        **more,
    )(*ins)


def dispatch_kernel(routes_t, pooled, out):
    tok = pooled.shape[0]
    shape = (out.shape[0], tok)
    row = iota(shape, 0)
    owner = row >> 1
    named = (owner == routes_t[0:1, :]) | (owner == routes_t[1:2, :])
    earlier = ones_where(iota((tok, tok), 0) < iota((tok, tok), 1))
    rank = dot(ones_where(named), earlier)
    first = (BLOCKS * (row & 1)).astype(F32)
    feature = pooled.shape[1]
    for c in range(BLOCKS):
        pick = ones_where(named & (rank == first + c))
        out[:, c * feature : (c + 1) * feature] = dot(pick, pooled[...]).astype(BF)


def prepare_kernel(
    routes, routes_t, pooled, gate_flat, bag_rows, bag_sample, take, put, gate_rows, gates, side, bag_pick
):
    tok = pooled.shape[0]
    rows = gate_flat.shape[0]
    row = iota((tok, rows), 1)
    named = [(row >> 1) == routes[:, k : k + 1] for k in range(2)]
    earlier = ones_where(iota((tok, tok), 0) > iota((tok, tok), 1))
    rank = dot(earlier, ones_where(named[0] | named[1]))
    first = (BLOCKS * (row & 1)).astype(F32)
    for k in range(2):
        for c in range(BLOCKS):
            take[BLOCKS * k + c] = ones_where(named[k] & (rank == first + c))
    row_t = iota((rows, tok), 0)
    named_t = [(row_t >> 1) == routes_t[k : k + 1, :] for k in range(2)]
    later = ones_where(iota((tok, tok), 0) < iota((tok, tok), 1))
    rank_t = dot(ones_where(named_t[0] | named_t[1]), later)
    first_t = (BLOCKS * (row_t & 1)).astype(F32)
    for k in range(2):
        for c in range(BLOCKS):
            put[BLOCKS * k + c] = ones_where(named_t[k] & (rank_t == first_t + c))
    logits = dot_last(pooled[...], gate_flat[...])
    lane = iota((tok, 128), 1)
    gate = jnp.zeros((tok, 128), F32)
    for t in range(2):
        of_task = (row & 1) == t
        chosen = [
            jnp.sum(jnp.where(named[k] & of_task, logits, 0.0), axis=1, keepdims=True)
            for k in range(2)
        ]
        gate = jnp.where(lane == t, jax.nn.sigmoid(chosen[0] - chosen[1]), gate)
        signs = jnp.where(named[0] & of_task, 1.0, jnp.where(named[1] & of_task, -1.0, 0.0))
        gate_rows[t] = dot(signs.astype(BF), gate_flat[...])
    gates[...] = gate
    numbers = jnp.zeros((rows, 128), jnp.int32)
    side_lane = iota((rows, 128), 1)
    for b in range(2):
        number = bag_rows[:, b : b + 1]
        numbers = jnp.where(side_lane == ROW_LANES + 2 * b, number >> 8, numbers)
        numbers = jnp.where(side_lane == ROW_LANES + 2 * b + 1, number & 255, numbers)
        bag_pick[b] = ones_where(bag_sample[:, b : b + 1] == iota((rows, tok), 1))
    side[...] = numbers.astype(F32)


def expert_kernel(x, w_in, w_out, tower, out, total):
    step = pl.program_id(0)
    rows = x.shape[0]
    feature = w_in.shape[1]
    wide = 3 * feature

    @pl.when(step == 0)
    def _():
        total[...] = jnp.zeros_like(total)

    slopes = dot_last(tower_pieces(tower[...]), w_out[...])
    slope = [slopes[t : t + 1] + slopes[2 + t : 3 + t] + slopes[4 + t : 5 + t] for t in range(2)]
    for c in range(BLOCKS):
        pre = dot_last(x[:, c * feature : (c + 1) * feature], w_in[...])
        act, grad = silu_and_slope(pre)
        at = c * wide
        total[:, at : at + feature] += dot(act.astype(BF), w_out[...])
        for t in range(2):
            cols = slice(at + (1 + t) * feature, at + (2 + t) * feature)
            total[:, cols] += dot((grad * slope[t]).astype(BF), w_in[...])

    @pl.when(step == pl.num_programs(0) - 1)
    def _():
        out[...] = total[...].astype(BF)


def half_kernel(half, x, x_other, w_in, w_out, tower, act_t, grad_t, slope):
    del half
    feature = w_in.shape[1]
    rows = x.shape[0]
    slopes = dot_last(w_out[...], tower_pieces(tower[...]))
    lane = iota(slope.shape, 1)
    wide = jnp.zeros(slope.shape, F32)
    for t in range(2):
        column = slopes[:, t : t + 1] + slopes[:, 2 + t : 3 + t] + slopes[:, 4 + t : 5 + t]
        wide = jnp.where(lane == t, column, wide)
    slope[...] = wide
    for r, source in enumerate((x, x_other)):
        for c in range(BLOCKS):
            pre = dot_last(w_in[...], source[:, c * feature : (c + 1) * feature])
            act, grad = silu_and_slope(pre)
            at = (BLOCKS * r + c) * rows
            act_t[:, at : at + rows] = act.astype(BF)
            grad_t[:, at : at + rows] = grad.astype(BF)


def sample_kernel(
    back, take, put, gate_rows, gates, side, bag_pick, labels, tower, bias, bag_weight, out
):
    feature = tower.shape[1]
    wide = 3 * feature
    parts = []
    for k in range(2):
        part = dot(take[BLOCKS * k], back[:, :wide])
        for c in range(1, BLOCKS):
            part += dot(take[BLOCKS * k + c], back[:, c * wide : (c + 1) * wide])
        parts.append(part)
    result = [part[:, :feature] for part in parts]
    gate, towers, first_grad = [], [], []
    pulls = [[None, None], [None, None]]
    for t in range(2):
        weight = tower[t : t + 1, :]
        along = [jnp.sum(result[k] * weight, axis=1, keepdims=True) for k in range(2)]
        first = gates[:, t : t + 1]
        second = 1.0 - first
        logit = first * along[0] + second * along[1] + bias[t]
        label = labels[:, t : t + 1].astype(F32)
        logit_grad = LOSS_SCALE * (jax.nn.sigmoid(logit) - label)
        pulls[0][t], pulls[1][t] = first * logit_grad, second * logit_grad
        first_grad.append(logit_grad * (along[0] - along[1]) * first * second)
        mixture = first * result[0] + second * result[1]
        towers.append(jnp.sum(logit_grad * mixture, axis=0, keepdims=True))
    pooled_grad = first_grad[0] * gate_rows[0] + first_grad[1] * gate_rows[1]
    for k in range(2):
        for t in range(2):
            pooled_grad += pulls[k][t] * parts[k][:, (1 + t) * feature : (2 + t) * feature]
    pieces = three_pieces(pooled_grad)
    for b in range(2):
        picked = sum(dot(bag_pick[b], piece) for piece in pieces)
        out[:, b * feature : (b + 1) * feature] = (bag_weight[:, b : b + 1] * picked).astype(BF)
    tok = gates.shape[0]
    lane = iota((tok, 128), 1)
    blocks = [None] * BLOCKS
    for k in range(2):
        sign = 1.0 if k == 0 else -1.0
        values = [pulls[k][0], pulls[k][1], sign * first_grad[0], sign * first_grad[1]]
        packed = jnp.zeros((tok, 128), F32)
        for v, value in enumerate(values):
            for p, piece in enumerate(three_pieces(value)):
                packed = jnp.where(lane == PIECES * v + p, piece.astype(F32), packed)
        packed = packed.astype(BF)
        for c in range(BLOCKS):
            placed = dot(put[BLOCKS * k + c], packed)
            blocks[c] = placed if blocks[c] is None else blocks[c] + placed
    extra = side[...] + blocks[0]
    for c in range(1, BLOCKS):
        extra += pltpu.roll(blocks[c], c * SLOT_LANES, 1)
    at = 2 * feature
    out[:, at : at + 128] = extra.astype(BF)
    task = iota((out.shape[0], feature), 0) & 1
    total = jnp.where(task == 0, towers[0], towers[1])
    high = total.astype(BF)
    at += 128
    out[:, at : at + feature] = high
    out[:, at + feature : at + 2 * feature] = (total - high.astype(F32)).astype(BF)


def final_kernel(
    x,
    x_other,
    got,
    got_other,
    act_t,
    grad_t,
    slope,
    tower,
    table,
    in_grad,
    out_grad,
    gate_grad,
    tower_grad,
    new_table,
    scaled,
    pulls,
    targets,
):
    feature = tower.shape[1]
    rows = x.shape[0]
    at_side = 2 * feature
    at_tower = at_side + 128
    step = pl.program_id(0)

    @pl.when(step == 0)
    def _():
        gate_total = [jnp.zeros((1, feature), F32) for _ in range(2)]
        tower_total = [jnp.zeros((1, feature), F32) for _ in range(2)]
        lane = iota((rows, 128), 1)
        task = iota((rows, feature), 0) & 1
        wanted = iota((8, 128), 1)
        asked = iota((8, 128), 0)
        select = jnp.zeros((8, 128), F32)
        for b in range(2):
            select = jnp.where((asked == b) & (wanted == ROW_LANES + 2 * b), 256.0, select)
            select = jnp.where((asked == b) & (wanted == ROW_LANES + 2 * b + 1), 1.0, select)
        for r, (inputs, source) in enumerate(((x, got), (x_other, got_other))):
            side = source[:, at_side : at_side + 128]
            targets[8 * r : 8 * r + 8, :] = dot_last(select.astype(BF), side)
            side = side.astype(F32)
            for c in range(BLOCKS):
                values = []
                packed = jnp.zeros((rows, 128), F32)
                for v in range(4):
                    start = c * SLOT_LANES + PIECES * v
                    pieces = [side[:, start + p : start + p + 1] for p in range(PIECES)]
                    values.append(pieces[0] + pieces[1] + pieces[2])
                    if v < 2:
                        for p, piece in enumerate(pieces):
                            packed = jnp.where(lane == PIECES * v + p, piece, packed)
                at = (BLOCKS * r + c) * rows
                pulls[at : at + rows, :] = packed.astype(BF)
                block = inputs[:, c * feature : (c + 1) * feature].astype(F32)
                for t in range(2):
                    cols = slice(t * feature, (t + 1) * feature)
                    scaled[at : at + rows, cols] = (values[t] * block).astype(BF)
                    gate_total[t] += jnp.sum(values[2 + t] * block, axis=0, keepdims=True)
            sent = source[:, at_tower : at_tower + feature].astype(F32)
            sent += source[:, at_tower + feature : at_tower + 2 * feature].astype(F32)
            for t in range(2):
                tower_total[t] += jnp.sum(jnp.where(task == t, sent, 0.0), axis=0, keepdims=True)
        for t in range(2):
            gate_grad[t : t + 1, :] = gate_total[t]
            tower_grad[t : t + 1, :] = tower_total[t]

    both = dot(grad_t[...], scaled[...])
    in_grad[...] = slope[:, 0:1] * both[:, :feature] + slope[:, 1:2] * both[:, feature:]
    along = dot(act_t[...], pulls[...])
    reach = [along[:, 3 * t : 3 * t + 1] + along[:, 3 * t + 1 : 3 * t + 2] + along[:, 3 * t + 2 : 3 * t + 3] for t in range(2)]
    out_grad[...] = reach[0] * tower[0:1, :] + reach[1] * tower[1:2, :]
    depth = table.shape[0]
    number = (step * depth + iota((depth, rows), 0)).astype(F32)
    sums = jnp.zeros(table.shape, F32)
    for r, source in enumerate((got, got_other)):
        for b in range(2):
            hit = ones_where(number == targets[8 * r + b : 8 * r + b + 1, :])
            sums += dot(hit, source[:, b * feature : (b + 1) * feature])
    new_table[...] = table[...] - STEP_SIZE * sums


def exchanged(rows):
    width = rows.shape[1]
    moved = lax.all_to_all(rows.reshape(-1, ROWS, width), EXPERT, split_axis=0, concat_axis=0, tiled=True)
    return moved.reshape(-1, width)


def swapped(shard):
    return lax.ppermute(shard, "dp", [(0, 1), (1, 0)])


def shapes(*items):
    return tuple(jax.ShapeDtypeStruct(shape, dtype) for shape, dtype in items)


def on_device(
    pooled,
    routes,
    labels,
    in_weight,
    out_weight,
    gate_weight,
    tower_weight,
    tower_bias,
    bag_rows,
    bag_sample,
    bag_weight,
    row_table,
):
    owners = lax.axis_size(EXPERT)
    tok, feature = pooled.shape
    hidden = in_weight.shape[1]
    half = hidden // lax.axis_size("dp")
    rows = ROWS * owners
    slots = 2 * BLOCKS * rows
    in_matrix, out_matrix = in_weight[0], out_weight[0]
    gate_flat = gate_weight.reshape(-1, feature)
    routes_t = routes.T
    vmem = pltpu.CompilerParams(vmem_limit_bytes=56 << 20)

    outbound = call(
        dispatch_kernel,
        jax.ShapeDtypeStruct((rows, BLOCKS * feature), BF),
        (routes_t, pooled),
        1 << 27,
        "dispatch",
    )
    received = exchanged(outbound)
    take, put, gate_rows, gates, side, bag_pick = call(
        prepare_kernel,
        shapes(
            ((2 * BLOCKS, tok, rows), BF),
            ((2 * BLOCKS, rows, tok), BF),
            ((2, tok, feature), F32),
            ((tok, 128), F32),
            ((rows, 128), F32),
            ((2, rows, tok), BF),
        ),
        (routes, routes_t, pooled, gate_flat, bag_rows.reshape(rows, 2), bag_sample.reshape(rows, 2)),
        1 << 31,
        "prepare",
    )
    depth = hidden // 4
    message = call(
        expert_kernel,
        jax.ShapeDtypeStruct((rows, 3 * BLOCKS * feature), BF),
        (received, in_matrix, out_matrix, tower_weight),
        7 << 30,
        "expert",
        grid=(hidden // depth,),
        in_specs=[
            full(received.shape),
            pl.BlockSpec((depth, feature), lambda i: (i, 0)),
            pl.BlockSpec((depth, feature), lambda i: (i, 0)),
            full(tower_weight.shape),
        ],
        out_specs=full((rows, 3 * BLOCKS * feature)),
        scratch_shapes=[pltpu.VMEM((rows, 3 * BLOCKS * feature), F32)],
        compiler_params=vmem,
    )
    returned = exchanged(message)
    received_other = swapped(received)
    tile = 256
    tiles = half // tile
    which = jnp.full((1,), lax.axis_index("dp"), jnp.int32)
    act_t, grad_t, slope = call(
        half_kernel,
        shapes(((half, slots), BF), ((half, slots), BF), ((half, 128), F32)),
        (which, received, received_other, in_matrix, out_matrix, tower_weight),
        7 << 30,
        "half",
        grid_spec=pltpu.PrefetchScalarGridSpec(
            num_scalar_prefetch=1,
            grid=(tiles,),
            in_specs=[
                full(received.shape),
                full(received.shape),
                pl.BlockSpec((tile, feature), lambda i, part: (part[0] * tiles + i, 0)),
                pl.BlockSpec((tile, feature), lambda i, part: (part[0] * tiles + i, 0)),
                full(tower_weight.shape),
            ],
            out_specs=[
                pl.BlockSpec((tile, slots), lambda i, part: (i, 0)),
                pl.BlockSpec((tile, slots), lambda i, part: (i, 0)),
                pl.BlockSpec((tile, 128), lambda i, part: (i, 0)),
            ],
        ),
        compiler_params=vmem,
    )
    width = 4 * feature + 128
    sent = call(
        sample_kernel,
        jax.ShapeDtypeStruct((rows, width), BF),
        (
            returned,
            take,
            put,
            gate_rows,
            gates,
            side,
            bag_pick,
            labels,
            tower_weight,
            tower_bias,
            bag_weight.reshape(rows, 2),
        ),
        1 << 29,
        "sample",
        in_specs=[pl.BlockSpec(memory_space=pltpu.VMEM)] * 9
        + [pl.BlockSpec(memory_space=pltpu.SMEM), pl.BlockSpec(memory_space=pltpu.VMEM)],
        compiler_params=vmem,
    )
    got = exchanged(sent)
    got_other = swapped(got)
    table_tile = row_table.shape[0] // tiles
    in_grad, out_grad, gate_grad, tower_grad, new_table = call(
        final_kernel,
        shapes(
            ((half, feature), F32),
            ((half, feature), F32),
            ((2, feature), F32),
            ((2, feature), F32),
            (row_table.shape, F32),
        ),
        (received, received_other, got, got_other, act_t, grad_t, slope, tower_weight, row_table),
        6 << 30,
        "final",
        grid=(tiles,),
        in_specs=[
            full(received.shape),
            full(received.shape),
            full(got.shape),
            full(got.shape),
            pl.BlockSpec((tile, slots), lambda i: (i, 0)),
            pl.BlockSpec((tile, slots), lambda i: (i, 0)),
            pl.BlockSpec((tile, 128), lambda i: (i, 0)),
            full(tower_weight.shape),
            pl.BlockSpec((table_tile, feature), lambda i: (i, 0)),
        ],
        out_specs=[
            pl.BlockSpec((tile, feature), lambda i: (i, 0)),
            pl.BlockSpec((tile, feature), lambda i: (i, 0)),
            full((2, feature)),
            full((2, feature)),
            pl.BlockSpec((table_tile, feature), lambda i: (i, 0)),
        ],
        scratch_shapes=[
            pltpu.VMEM((slots, 2 * feature), BF),
            pltpu.VMEM((slots, 128), BF),
            pltpu.VMEM((16, rows), F32),
        ],
        compiler_params=vmem,
    )
    return (in_grad[None], out_grad[None], gate_grad[None], tower_grad, new_table)


def solution(mesh):
    split = Mesh(
        mesh.devices.reshape(4, 8, 4, mesh.shape["dp"]), ("expert_0", "expert_1", "expert_2", "dp")
    )
    in_specs = (
        P(EXPERT_DP, None),
        P(EXPERT_DP, None),
        P(EXPERT_DP, None),
        P(EXPERT, None, None),
        P(EXPERT, None, None),
        P(),
        P(),
        P(),
        P(EXPERT_DP),
        P(EXPERT_DP),
        P(EXPERT_DP),
        P(EXPERT, None),
    )
    out_specs = (
        P(EXPERT, "dp", None),
        P(EXPERT, "dp", None),
        P(EXPERT, None, None),
        P(),
        P(EXPERT, None),
    )
    return jax.shard_map(
        on_device, mesh=split, in_specs=in_specs, out_specs=out_specs, check_vma=False
    )
```

profile of v0, /device:TPU:1, one launch (start us, length us, event | category | flops | bytes accessed | tf_op | source)
XLA Modules:
  0.0 156.6 jit_solution(405617472312880056)
XLA Ops:
  0.6 2.1 %dispatch.1 = bf16[256,768]{1,0:T(8,128)(2,1)} custom-call(s32[2,256]{1,0:T(2,128)} %bitcast.7, bf16[256,256]{1,0:T(8,128)(2,1)} %pooled.3), custom_call_target="tpu_custom_call" | custom-call | flops 134217728 | bytes 1048576 | tf_op jit(solution)/shard_map/dispatch/pallas_call | solution.py:71
  2.7 1.1 reshape.40
  3.9 31.0 %all_to_all.15 = bf16[128,2,768]{2,1,0:T(2,128)(2,1)S(1)} all-to-all(bf16[128,2,768]{2,1,0:T(2,128)(2,1)S(1)} %reshape.40), channel_id=1, replica_groups=mesh['expert_0'=4,'expert_1'=8,'expert_2'=4,'dp'=2] {'expert_0','expert_..., dimensions={0} | all-to-all | bytes 786432 | tf_op jit(solution)/shard_map/all_to_all | solution.py:329
  34.9 0.9 reshape.41.x
  35.8 12.3 %expert.1 = bf16[256,2304]{1,0:T(8,128)(2,1)} custom-call(bf16[256,768]{1,0:T(8,128)(2,1)} %reshape.41.x, bf16[4096,256]{1,0:T(8,128)(2,1)} %bitcast.9, bf16[4096,256]{1,0:T(8,128)(2,1)} %bitcast.11, f32[2,256]{1,0:T(2,128)} %tower.7), custom_call_target="tpu_custom_call" | custom-call | flops 7516192768 | bytes 1048576 | tf_op jit(solution)/shard_map/expert/pallas_call | solution.py:71
  48.0 0.0 copy-start.5
  48.0 3.6 %reshape.42 = bf16[128,2,2304]{2,1,0:T(2,128)(2,1)} reshape(bf16[256,2304]{1,0:T(8,128)(2,1)} %expert.1) | data formatting | bytes 2359296 | tf_op jit(solution)/shard_map/reshape | solution.py:329
  51.7 8.0 %all-to-all-start.1 = ((bf16[128,2,2304]{2,1,0:T(2,128)(2,1)}), bf16[128,2,2304]{2,1,0:T(2,128)(2,1)S(1)}, u32[]{:S(2)}, u32[]{:S(2)}) async-start(bf16[128,2,2304]{2,1,0:T(2,128)(2,1)} %reshape.42), calls=%async_computation.1 | async-start | bytes 2359296 | tf_op jit(solution)/shard_map/all_to_all | solution.py:329
  59.7 0.8 copy.19.routes
  60.5 0.8 copy.20.labels
  61.3 0.0 copy-done.2
  61.3 0.7 reshape.44.gate_flat
  62.0 0.8 reshape.45.bag_rows
  62.8 0.8 reshape.46.bag_sample
  63.6 0.8 reshape.47.bag_weight
  64.4 3.2 %prepare.1 = (bf16[6,256,256]{2,1,0:T(8,128)(2,1)}, bf16[6,256,256]{2,1,0:T(8,128)(2,1)}, f32[2,256,256]{2,1,0:T(8,128)}, f32[256,128]{1,0:T(8,128)}, f32[256,128]{1,0:T(8,128)}, /*index=5*/bf16[2,256,256]{2,1,0:T(8,128)(2,1)}) custom-call(s32[256,2]{1,0:T(8,128)} %copy.19.routes, s32[2,256]{1,0:T(2,128)} %bitcast.8, bf16[256,256]{1,0:T(8,128)(2,1)} %pooled.3, ...), custom_call_target="tpu_custom_call" | custom-call | flops 2147483648 | bytes 1048576 | tf_op jit(solution)/shard_map/prepare/pallas_call | solution.py:71
  67.6 20.8 %all-to-all-done.1 = bf16[128,2,2304]{2,1,0:T(2,128)(2,1)S(1)} async-done(((bf16[128,2,2304]{2,1,0:T(2,128)(2,1)}), bf16[128,2,2304]{2,1,0:T(2,128)(2,1)S(1)}, u32[]{:S(2)}, u32[]{:S(2)}) %all-to-all-start.1) | async-done | bytes 1179680 | tf_op jit(solution)/shard_map/all_to_all | solution.py:329
  88.4 1.3 reshape.43.back
  89.7 5.2 %sample.1 = bf16[256,1152]{1,0:T(8,128)(2,1)} custom-call(bf16[256,2304]{1,0:T(8,128)(2,1)} %reshape.43.back, bf16[6,256,256]{2,1,0:T(8,128)(2,1)} %get-tuple-element.19.take, bf16[6,256,256]{2,1,0:T(8,128)(2,1)} %get-tuple-element.20.put, f32[2,256,256]{2,1,0:T(8,128)} %get-tuple-element.21.gate_rows, f32[256,128]{1,0:T(8,128)} %get-tuple-element.22.gates, ...), custom_call_target="tpu_custom_call" | custom-call | flops 536870912 | bytes 1048576 | tf_op jit(solution)/shard_map/sample/pallas_call | solution.py:71
  94.9 2.6 %reshape.48 = bf16[128,2,1152]{2,1,0:T(2,128)(2,1)} reshape(bf16[256,1152]{1,0:T(8,128)(2,1)} %sample.1) | data formatting | bytes 1179648 | tf_op jit(solution)/shard_map/reshape | solution.py:329
  97.5 9.3 %all-to-all-start.2 = ((bf16[128,2,1152]{2,1,0:T(2,128)(2,1)}), bf16[128,2,1152]{2,1,0:T(2,128)(2,1)S(1)}, u32[]{:S(2)}, u32[]{:S(2)}) async-start(bf16[128,2,1152]{2,1,0:T(2,128)(2,1)} %reshape.48), calls=%async_computation.2 | async-start | bytes 1179648 | tf_op jit(solution)/shard_map/all_to_all | solution.py:329
  106.9 2.7 %collective-permute-start = (bf16[256,768]{1,0:T(8,128)(2,1)S(1)}, bf16[256,768]{1,0:T(8,128)(2,1)S(1)}, u32[]{:S(2)}, u32[]{:S(2)}) collective-permute-start(bf16[256,768]{1,0:T(8,128)(2,1)S(1)} %copy-done.1), channel_id=1, source_target_pairs={{0,1},{1,0},{2,3},{3,2},{4,5},{5,4},{6,7},{7,6},{8,9},{9,8},{10,11... | collective-permute-start | bytes 1179656 | tf_op jit(solution)/shard_map/ppermute | solution.py:334
  109.6 13.5 %all-to-all-done.2 = bf16[128,2,1152]{2,1,0:T(2,128)(2,1)S(1)} async-done(((bf16[128,2,1152]{2,1,0:T(2,128)(2,1)}), bf16[128,2,1152]{2,1,0:T(2,128)(2,1)S(1)}, u32[]{:S(2)}, u32[]{:S(2)}) %all-to-all-start.2) | async-done | bytes 589856 | tf_op jit(solution)/shard_map/all_to_all | solution.py:329
  123.1 0.2 reshape.49.got
  123.3 5.5 %collective-permute-start.1 = (bf16[256,1152]{1,0:T(8,128)(2,1)S(1)}, bf16[256,1152]{1,0:T(8,128)(2,1)S(1)}, u32[]{:S(2)}, u32[]{:S(2)}) collective-permute-start(bf16[256,1152]{1,0:T(8,128)(2,1)S(1)} %reshape.49.got), channel_id=1, source_target_pairs={{0,1},{1,0},{2,3},{3,2},{4,5},{5,4},{6,7},{7,6},{8,9},{9,8},{10,11... | collective-permute-start | bytes 1769480 | tf_op jit(solution)/shard_map/ppermute | solution.py:334
  128.8 0.0 collective-permute-done.x_other
  128.8 0.8 copy-done.9
  129.6 10.5 %half.1 = (bf16[2048,1536]{1,0:T(8,128)(2,1)}, bf16[2048,1536]{1,0:T(8,128)(2,1)}, f32[2048,128]{1,0:T(8,128)}) custom-call(s32[1]{0:T(128)} %bitcast.3.half, bf16[256,768]{1,0:T(8,128)(2,1)} %reshape.41.x, bf16[256,768]{1,0:T(8,128)(2,1)} %copy-done.9, bf16[4096,256]{1,0:T(8,128)(2,1)} %bitcast.10, bf16[4096,256]{1,0:T(8,128)(2,1)} %bitcast.12, f32[2,256]{1,0:T(2,128)} %tower.7), custom_call_target="tpu_custom_call" | custom-call | flops 7516192768 | bytes 1048576 | tf_op jit(solution)/shard_map/half/pallas_call | solution.py:71
  140.1 0.0 copy-done
  140.1 0.0 collective-permute-done.1.got_other
  140.1 0.8 copy-done.8
  140.9 15.5 %final.1 = (f32[2048,256]{1,0:T(8,128)}, f32[2048,256]{1,0:T(8,128)}, f32[2,256]{1,0:T(2,128)}, f32[2,256]{1,0:T(2,128)}, f32[1024,256]{1,0:T(8,128)}) custom-call(bf16[256,768]{1,0:T(8,128)(2,1)} %reshape.41.x, bf16[256,768]{1,0:T(8,128)(2,1)} %copy-done.9, bf16[256,1152]{1,0:T(8,128)(2,1)} %copy-done, bf16[256,1152]{1,0:T(8,128)(2,1)} %copy-done.8, ...), custom_call_target="tpu_custom_call" | custom-call | flops 6442450944 | bytes 1048576 | tf_op jit(solution)/shard_map/final/pallas_call | solution.py:71
  (15 shorter events, 0.0 us)
Async XLA Ops:
  48.0 11.6 %copy-start.3 = (s32[256,2]{0,1:T(2,128)S(1)}, s32[256,2]{0,1:T(2,128)}, u32[]{:S(2)}) copy-start(s32[256,2]{0,1:T(2,128)} %param.13) | copy-start | bytes 6148
  48.0 12.5 %copy-start.4 = (s32[256,2]{0,1:T(2,128)S(1)}, s32[256,2]{0,1:T(2,128)}, u32[]{:S(2)}) copy-start(s32[256,2]{0,1:T(2,128)} %param.14) | copy-start | bytes 6148
  48.0 13.3 %copy-start.2 = (bf16[128,2,256]{2,1,0:T(2,128)(2,1)S(1)}, bf16[128,2,256]{2,1,0:T(2,128)(2,1)}, u32[]{:S(2)}) copy-start(bf16[128,2,256]{2,1,0:T(2,128)(2,1)} %param.17) | copy-start | bytes 393220
  48.0 14.0 %copy-start.5 = (s32[512]{0:T(512)S(1)}, s32[512]{0:T(512)}, u32[]{:S(2)}) copy-start(s32[512]{0:T(512)} %param.20) | copy-start | bytes 6148
  51.7 11.1 %copy-start.6 = (s32[512]{0:T(512)S(1)}, s32[512]{0:T(512)}, u32[]{:S(2)}) copy-start(s32[512]{0:T(512)} %param.21) | copy-start | bytes 6148
  51.7 11.9 %copy-start.7 = (f32[512]{0:T(512)S(1)}, f32[512]{0:T(512)}, u32[]{:S(2)}) copy-start(f32[512]{0:T(512)} %param.22) | copy-start | bytes 6148
  51.7 36.8 %all-to-all-start.1 = ((bf16[128,2,2304]{2,1,0:T(2,128)(2,1)}), bf16[128,2,2304]{2,1,0:T(2,128)(2,1)S(1)}, u32[]{:S(2)}, u32[]{:S(2)}) async-start(bf16[128,2,2304]{2,1,0:T(2,128)(2,1)} %reshape.42), calls=%async_computation.1 | async-start | bytes 2359296 | tf_op jit(solution)/shard_map/all_to_all | solution.py:329
  94.9 12.0 %copy-start.1 = (bf16[256,768]{1,0:T(8,128)(2,1)S(1)}, bf16[256,768]{1,0:T(8,128)(2,1)}, u32[]{:S(2)}) copy-start(bf16[256,768]{1,0:T(8,128)(2,1)} %reshape.41.x) | copy-start | bytes 1179652
  97.5 25.6 %all-to-all-start.2 = ((bf16[128,2,1152]{2,1,0:T(2,128)(2,1)}), bf16[128,2,1152]{2,1,0:T(2,128)(2,1)S(1)}, u32[]{:S(2)}, u32[]{:S(2)}) async-start(bf16[128,2,1152]{2,1,0:T(2,128)(2,1)} %reshape.48), calls=%async_computation.2 | async-start | bytes 1179648 | tf_op jit(solution)/shard_map/all_to_all | solution.py:329
  106.9 22.0 %collective-permute-start = (bf16[256,768]{1,0:T(8,128)(2,1)S(1)}, bf16[256,768]{1,0:T(8,128)(2,1)S(1)}, u32[]{:S(2)}, u32[]{:S(2)}) collective-permute-start(bf16[256,768]{1,0:T(8,128)(2,1)S(1)} %copy-done.1), channel_id=1, source_target_pairs={{0,1},{1,0},{2,3},{3,2},{4,5},{5,4},{6,7},{7,6},{8,9},{9,8},{10,11... | collective-permute-start | bytes 1179656 | tf_op jit(solution)/shard_map/ppermute | solution.py:334
  123.3 16.8 %copy-start = (bf16[256,1152]{1,0:T(8,128)(2,1)}, bf16[256,1152]{1,0:T(8,128)(2,1)S(1)}, u32[]{:S(2)}) copy-start(bf16[256,1152]{1,0:T(8,128)(2,1)S(1)} %reshape.49.got) | copy-start | bytes 1769476
  123.3 16.8 %collective-permute-start.1 = (bf16[256,1152]{1,0:T(8,128)(2,1)S(1)}, bf16[256,1152]{1,0:T(8,128)(2,1)S(1)}, u32[]{:S(2)}, u32[]{:S(2)}) collective-permute-start(bf16[256,1152]{1,0:T(8,128)(2,1)S(1)} %reshape.49.got), channel_id=1, source_target_pairs={{0,1},{1,0},{2,3},{3,2},{4,5},{5,4},{6,7},{7,6},{8,9},{9,8},{10,11... | collective-permute-start | bytes 1769480 | tf_op jit(solution)/shard_map/ppermute | solution.py:334
  128.8 0.8 copy-start.9
  140.1 0.8 copy-start.8
where the time goes:
time: 158 us; the launch traced here: 157 us
  Pallas kernels  48.8 us (31%)
  waiting for transfers between devices  34.3 us (22%)
  blocking collectives  31 us (20%)
  starting transfers between devices  25.5 us (16%)
  local copies, waits for them, and re-layouts  16.1 us (10%)
    pallas_call x6, Pallas kernels, call(): pl.pallas_call(kernel, out_shape=out_shape, cost_estimate=pl.CostEstimate...  48.8 us
    all_to_all x2, waiting for transfers between devices, exchanged(): lax.all_to_all(rows.reshape(-1, ROWS, width), EXPERT, split_axis=0, conca...  34.3 us
    all_to_all x1, blocking collectives, exchanged(): lax.all_to_all(rows.reshape(-1, ROWS, width), EXPERT, split_axis=0, conca...  31 us
    all_to_all x2, starting transfers between devices, exchanged(): lax.all_to_all(rows.reshape(-1, ROWS, width), EXPERT, split_axis=0, conca...  17.3 us
    ppermute x2, starting transfers between devices, swapped(): return lax.ppermute(shard, 'dp', [(0, 1), (1, 0)])  8.2 us
    reshape x3, local copies, waits for them, and re-layouts, exchanged(): rows.reshape(-1, ROWS, width)  7.39 us
    unnamed x22, local copies, waits for them, and re-layouts  3.22 us
  transfers between devices with their start and end apart: 4, of which 2 were waited for; matrix products, arithmetic and copies ran while one was open for 3% of the time, Pallas kernels for 9%

commit v1 on v0

v1 whole, which is shorter than its diff:
```python
import functools

import jax
import jax.numpy as jnp
from jax import lax
from jax.experimental import pallas as pl
from jax.experimental.pallas import tpu as pltpu
from jax.sharding import Mesh
from jax.sharding import PartitionSpec as P

EXPERT = ("expert_0", "expert_1", "expert_2")
EXPERT_DP = ("expert_0", "expert_1", "expert_2", "dp")

LOSS_SCALE = 32.0
STEP_SIZE = 0.25
BF = jnp.bfloat16
F32 = jnp.float32
CHUNK = 2048

ROWS = 2
BLOCKS = 3
PIECES = 3
SLOT_LANES = 4 * PIECES
SLOTS = ROWS * BLOCKS
ROW_LANES = SLOTS * SLOT_LANES
ENTRIES = 4
SIDE_ROW = 4
TOWER_ROW = 5


def dot(left, right):
    return jnp.dot(left, right, preferred_element_type=F32)


def dot_last(left, right):
    return lax.dot_general(left, right, (((1,), (1,)), ((), ())), preferred_element_type=F32)


def iota(shape, dim):
    return lax.broadcasted_iota(jnp.int32, shape, dim)


def ones_where(mask):
    return jnp.where(mask, 1.0, 0.0).astype(BF)


def three_pieces(value):
    high = value.astype(BF)
    rest = value - high.astype(F32)
    middle = rest.astype(BF)
    low = (rest - middle.astype(F32)).astype(BF)
    return high, middle, low


def tower_pieces(tower):
    pieces = three_pieces(tower)
    row = iota((8, tower.shape[1]), 0)
    stacked = jnp.zeros((8, tower.shape[1]), F32)
    for p, piece in enumerate(pieces):
        for t in range(2):
            stacked = jnp.where(row == 2 * p + t, piece[t : t + 1].astype(F32), stacked)
    return stacked.astype(BF)


def silu_and_slope(pre):
    sigma = 0.5 * jnp.tanh(0.5 * pre) + 0.5
    act = pre * sigma
    return act, sigma + act * (1.0 - sigma)


def full(shape):
    return pl.BlockSpec(shape, lambda *_: (0,) * len(shape))


def call(kernel, out_shape, ins, flops, name, mib, **more):
    return pl.pallas_call(
        kernel,
        out_shape=out_shape,
        cost_estimate=pl.CostEstimate(flops=flops, transcendentals=0, bytes_accessed=1 << 20),
        name=name,
        compiler_params=pltpu.CompilerParams(vmem_limit_bytes=mib << 20),
        **more,
    )(*ins)


def dispatch_kernel(routes_far, pooled_far, out, routes_t, pooled, sems):
    pairs = ((routes_far, routes_t), (pooled_far, pooled))
    copies = [pltpu.make_async_copy(far, near, sems.at[m]) for m, (far, near) in enumerate(pairs)]
    for copy in copies:
        copy.start()
    tok = pooled.shape[0]
    copies[0].wait()
    shape = (out.shape[0], tok)
    row = iota(shape, 0)
    owner = row >> 1
    named = (owner == routes_t[0:1, :]) | (owner == routes_t[1:2, :])
    earlier = ones_where(iota((tok, tok), 0) < iota((tok, tok), 1))
    rank = dot(ones_where(named), earlier)
    first = (BLOCKS * (row & 1)).astype(F32)
    feature = pooled.shape[1]
    copies[1].wait()
    for c in range(BLOCKS):
        pick = ones_where(named & (rank == first + c))
        out[:, c * feature : (c + 1) * feature] = dot(pick, pooled[...]).astype(BF)


def prepare_kernel(
    routes, routes_t, pooled, gate_flat, labels, bag_rows, bag_sample, bag_weight,
    take, put, gate_rows, lanes, side, bag_pick, bag_scale,
):
    tok = pooled.shape[0]
    rows = gate_flat.shape[0]
    owners = bag_rows.shape[0]
    row = iota((tok, rows), 1)
    named = [(row >> 1) == routes[:, k : k + 1] for k in range(2)]
    earlier = ones_where(iota((tok, tok), 0) > iota((tok, tok), 1))
    rank = dot(earlier, ones_where(named[0] | named[1]))
    first = (BLOCKS * (row & 1)).astype(F32)
    for k in range(2):
        for c in range(BLOCKS):
            take[BLOCKS * k + c] = ones_where(named[k] & (rank == first + c))
    owner = iota((owners, tok), 0)
    named_t = [owner == routes_t[k : k + 1, :] for k in range(2)]
    later = ones_where(iota((tok, tok), 0) < iota((tok, tok), 1))
    rank_t = dot(ones_where(named_t[0] | named_t[1]), later)
    for k in range(2):
        for j in range(SLOTS):
            put[SLOTS * k + j] = ones_where(named_t[k] & (rank_t == float(j)))
    logits = dot_last(pooled[...], gate_flat[...])
    lane = iota((tok, 128), 1)
    gate = jnp.zeros((tok, 128), F32)
    label = jnp.zeros((tok, 128), F32)
    for t in range(2):
        of_task = (row & 1) == t
        chosen = [
            jnp.sum(jnp.where(named[k] & of_task, logits, 0.0), axis=1, keepdims=True)
            for k in range(2)
        ]
        gate = jnp.where(lane == t, jax.nn.sigmoid(chosen[0] - chosen[1]), gate)
        label = jnp.where(lane == t, labels[:, t : t + 1].astype(F32), label)
        signs = jnp.where(named[0] & of_task, 1.0, jnp.where(named[1] & of_task, -1.0, 0.0))
        gate_rows[t] = dot(signs.astype(BF), gate_flat[...])
    lanes[0] = gate
    lanes[1] = label
    numbers = jnp.zeros((owners, 128), jnp.int32)
    side_lane = iota((owners, 128), 1)
    for r in range(ENTRIES):
        number = bag_rows[:, r : r + 1]
        numbers = jnp.where(side_lane == ROW_LANES + 2 * r, number >> 8, numbers)
        numbers = jnp.where(side_lane == ROW_LANES + 2 * r + 1, number & 255, numbers)
    side[...] = numbers.astype(F32)
    tall = bag_pick.shape[0]
    spread = ones_where((iota((tall, owners), 0) >> 3) == iota((tall, owners), 1))
    entry = iota((tall, ENTRIES), 0) & 7
    mine = entry == iota((tall, ENTRIES), 1)

    def column(value):
        spread_out = sum(dot(spread, piece) for piece in three_pieces(value))
        return jnp.sum(jnp.where(mine, spread_out, 0.0), axis=1, keepdims=True)

    sample = column(bag_sample[...].astype(F32))
    tall_iota = iota((tall, tok), 0) & 7
    hit = (sample == iota((tall, tok), 1).astype(F32)) & (tall_iota < ENTRIES)
    bag_pick[...] = ones_where(hit)
    bag_scale[...] = jnp.broadcast_to(column(bag_weight[...]), bag_scale.shape)


def slope_kernel(w_out, tower, slopes):
    found = dot_last(tower_pieces(tower[...]), w_out[...])
    for t in range(2):
        slopes[t : t + 1, :] = found[t : t + 1] + found[2 + t : 3 + t] + found[4 + t : 5 + t]


def expert_kernel(x, w_in, w_out_far, slopes, after, out, total, stacked, w_out, sems):
    del after
    rows = x.shape[0]
    hidden, feature = w_out.shape
    wide = 3 * feature
    units = [slice(at, at + CHUNK) for at in range(0, hidden, CHUNK)]
    arrived = []
    for n, unit in enumerate(units):
        copy = pltpu.make_async_copy(w_out_far.at[unit, :], w_out.at[unit, :], sems.at[n])
        copy.start()
        arrived.append(copy)
    for c in range(BLOCKS):
        stacked[c * rows : (c + 1) * rows, :] = x[:, c * feature : (c + 1) * feature]
    for n, unit in enumerate(units):
        act, grad = silu_and_slope(dot_last(stacked[...], w_in[unit, :]))
        parts = [
            dot((grad * slopes[t : t + 1, unit]).astype(BF), w_in[unit, :]) for t in range(2)
        ]
        act = act.astype(BF)
        arrived[n].wait()
        parts = [dot(act, w_out[unit, :])] + parts
        for p, part in enumerate(parts):
            cols = slice(p * feature, (p + 1) * feature)
            if n == 0:
                total[:, cols] = part
            else:
                total[:, cols] += part
    for c in range(BLOCKS):
        out[:, c * wide : (c + 1) * wide] = total[c * rows : (c + 1) * rows, :].astype(BF)


def half_kernel(half, x, x_other, w_in, w_out, tower, act_t, grad_t, slope):
    del half
    feature = w_in.shape[1]
    rows = x.shape[0]
    slopes = dot_last(w_out[...], tower_pieces(tower[...]))
    lane = iota(slope.shape, 1)
    wide = jnp.zeros(slope.shape, F32)
    for t in range(2):
        column = slopes[:, t : t + 1] + slopes[:, 2 + t : 3 + t] + slopes[:, 4 + t : 5 + t]
        wide = jnp.where(lane == t, column, wide)
    slope[...] = wide
    for r, source in enumerate((x, x_other)):
        for c in range(BLOCKS):
            pre = dot_last(w_in[...], source[:, c * feature : (c + 1) * feature])
            act, grad = silu_and_slope(pre)
            at = (BLOCKS * r + c) * rows
            act_t[:, at : at + rows] = act.astype(BF)
            grad_t[:, at : at + rows] = grad.astype(BF)


def sample_kernel(
    back, take, put_far, gate_rows_far, lanes_far, side_far, bag_pick_far, bag_scale_far,
    tower, bias, after,
    out, put, gate_rows, lanes, side, bag_pick, bag_scale, sems,
):
    del after
    pairs = (
        (lanes_far, lanes),
        (gate_rows_far, gate_rows),
        (bag_pick_far, bag_pick),
        (bag_scale_far, bag_scale),
        (put_far, put),
        (side_far, side),
    )
    copies = [pltpu.make_async_copy(far, near, sems.at[m]) for m, (far, near) in enumerate(pairs)]
    for copy in copies:
        copy.start()
    feature = tower.shape[1]
    wide = 3 * feature
    parts = []
    for k in range(2):
        part = dot(take[BLOCKS * k], back[:, :wide])
        for c in range(1, BLOCKS):
            part += dot(take[BLOCKS * k + c], back[:, c * wide : (c + 1) * wide])
        parts.append(part)
    task_row = iota((128, feature), 0)
    weights = [
        jnp.where(task_row == 0, piece[0:1].astype(F32), jnp.where(task_row == 1, piece[1:2].astype(F32), 0.0)).astype(BF)
        for piece in three_pieces(tower[...])
    ]
    along = []
    for k in range(2):
        result = parts[k][:, :feature].astype(BF)
        along.append(sum(dot_last(result, weight) for weight in weights))
    for copy in copies:
        copy.wait()
    first, label = lanes[0], lanes[1]
    second = 1.0 - first
    lane = iota(first.shape, 1)
    lane_bias = jnp.where(lane == 0, bias[0], bias[1])
    logit = first * along[0] + second * along[1] + lane_bias
    logit_grad = jnp.where(lane < 2, LOSS_SCALE * (jax.nn.sigmoid(logit) - label), 0.0)
    pulls = [first * logit_grad, second * logit_grad]
    first_grad = logit_grad * (along[0] - along[1]) * first * second
    pooled_grad = first_grad[:, 0:1] * gate_rows[0] + first_grad[:, 1:2] * gate_rows[1]
    towers = [0.0, 0.0]
    for k in range(2):
        for t in range(2):
            pull = jnp.broadcast_to(pulls[k][:, t : t + 1], (first.shape[0], feature))
            pooled_grad += pull * parts[k][:, (1 + t) * feature : (2 + t) * feature]
            towers[t] += jnp.sum(pull * parts[k][:, :feature], axis=0, keepdims=True)
    picked = sum(dot(bag_pick[...], piece) for piece in three_pieces(pooled_grad))
    placed = [None] * SLOTS
    for k in range(2):
        signed = first_grad if k == 0 else -first_grad
        packed = 0.0
        for kind, value in enumerate((pulls[k], signed)):
            for p, piece in enumerate(three_pieces(value)):
                piece = piece.astype(F32)
                shift = 2 * PIECES * kind + 2 * p
                packed += pltpu.roll(piece, shift, 1) if shift else piece
        packed = packed.astype(BF)
        for j in range(SLOTS):
            part = dot(put[SLOTS * k + j], packed)
            placed[j] = part if k == 0 else placed[j] + part
    extra = side[...] + placed[0]
    for j in range(1, SLOTS):
        extra += pltpu.roll(placed[j], j * SLOT_LANES, 1)
    tall, owners = bag_pick.shape[0], side.shape[0]
    spread = ones_where(iota((tall, owners), 0) == 8 * iota((tall, owners), 1) + SIDE_ROW)
    extra = dot(spread, extra.astype(BF))
    which = iota((tall, 128), 0) & 7
    for at in range(0, feature, 128):
        cols = slice(at, at + 128)
        value = bag_scale[...] * picked[:, cols]
        for t in range(2):
            value = jnp.where(which == TOWER_ROW + t, towers[t][:, cols], value)
        out[:, cols] = (value + extra if at == 0 else value).astype(BF)


def final_kernel(
    x,
    x_other,
    got,
    got_other,
    act_far,
    grad_far,
    slope,
    tower,
    table,
    in_grad,
    out_grad,
    gate_grad,
    tower_grad,
    new_table,
    scaled,
    routed,
    targets,
    act_t,
    grad_t,
    sems,
):
    feature = tower.shape[1]
    rows = x.shape[0]
    tall = got.shape[0]
    step = pl.program_id(0)
    tile = in_grad.shape[0]

    def arriving(n):
        part = pl.ds(n * tile, tile)
        pairs = ((grad_far, grad_t), (act_far, act_t))
        return [
            pltpu.make_async_copy(far.at[part, :], near.at[part, :], sems.at[m, n])
            for m, (far, near) in enumerate(pairs)
        ]

    @pl.when(step == 0)
    def _():
        for n in range(act_t.shape[0] // tile):
            for copy in arriving(n):
                copy.start()
        gate_total = [jnp.zeros((1, feature), F32) for _ in range(2)]
        tower_total = jnp.zeros((8, feature), F32)
        row = iota((rows, tall), 0)
        expand = ones_where(iota((rows, tall), 1) == 8 * (row >> 1) + SIDE_ROW)
        lane = iota((rows, 128), 1)
        half_lanes = BLOCKS * SLOT_LANES
        odd = (iota((rows, 128), 0) & 1) == 1
        own = (odd & (lane >= half_lanes) & (lane < ROW_LANES)) | (~odd & (lane < half_lanes))
        source_lane = iota((128, feature), 0)
        within = jnp.where(source_lane >= half_lanes, source_lane - half_lanes, source_lane)
        gather = {}
        for c in range(BLOCKS):
            for v in range(4):
                base = c * SLOT_LANES + 2 * PIECES * (v // 2) + v % 2
                gather[c, v] = ones_where((within == base) | (within == base + 2) | (within == base + 4))
        wanted, asked = iota((8, 128), 1), iota((8, 128), 0)
        select = jnp.where(wanted == ROW_LANES + 2 * asked, 256.0, 0.0)
        select = jnp.where(wanted == ROW_LANES + 2 * asked + 1, 1.0, select).astype(BF)
        which = iota((1, tall), 1) & 7
        tower_pick = ones_where((iota((8, tall), 1) & 7) == TOWER_ROW + iota((8, tall), 0))
        for r, (inputs, source) in enumerate(((x, got), (x_other, got_other))):
            numbers = dot_last(select, source[:, :128])
            target = jnp.full((1, tall), -1.0, F32)
            for e in range(ENTRIES):
                moved = pltpu.roll(numbers, tall + e - SIDE_ROW if e < SIDE_ROW else 0, 1)
                target = jnp.where(which == e, moved[e : e + 1], target)
            targets[8 * r : 8 * r + 8, :] = jnp.broadcast_to(target, (8, tall))
            tower_total += dot(tower_pick, source[...])
            side = jnp.where(own, dot(expand, source[:, :128]), 0.0).astype(BF)
            for c in range(BLOCKS):
                values = [dot(side, gather[c, v]) for v in range(4)]
                at = (BLOCKS * r + c) * rows
                block = inputs[:, c * feature : (c + 1) * feature].astype(F32)
                routed[at : at + rows, :] = (
                    values[0] * tower[0:1, :] + values[1] * tower[1:2, :]
                ).astype(BF)
                for t in range(2):
                    cols = slice(t * feature, (t + 1) * feature)
                    scaled[at : at + rows, cols] = (values[t] * block).astype(BF)
                    gate_total[t] += jnp.sum(values[2 + t] * block, axis=0, keepdims=True)
        for t in range(2):
            gate_grad[t : t + 1, :] = gate_total[t]
            tower_grad[t : t + 1, :] = tower_total[t : t + 1]

    for copy in arriving(step):
        copy.wait()
    part = pl.ds(pl.multiple_of(step * tile, tile), tile)
    both = dot(grad_t[part, :], scaled[...])
    in_grad[...] = slope[:, 0:1] * both[:, :feature] + slope[:, 1:2] * both[:, feature:]
    out_grad[...] = dot(act_t[part, :], routed[...])
    depth = table.shape[0]
    number = (step * depth + iota((depth, tall), 0)).astype(F32)
    sums = jnp.zeros(table.shape, F32)
    for r, source in enumerate((got, got_other)):
        sums += dot(ones_where(number == targets[8 * r : 8 * r + 1, :]), source[...])
    new_table[...] = table[...] - STEP_SIZE * sums


def exchanged(rows, each):
    width = rows.shape[1]
    moved = lax.all_to_all(rows.reshape(-1, each, width), EXPERT, split_axis=0, concat_axis=0, tiled=True)
    return moved.reshape(-1, width)


def swapped(shard):
    return lax.ppermute(shard, "dp", [(0, 1), (1, 0)])


def far(array):
    return pltpu.with_memory_space_constraint(array, pltpu.HBM)


def shapes(*items):
    return tuple(jax.ShapeDtypeStruct(shape, dtype) for shape, dtype in items)


def on_device(
    pooled,
    routes,
    labels,
    in_weight,
    out_weight,
    gate_weight,
    tower_weight,
    tower_bias,
    bag_rows,
    bag_sample,
    bag_weight,
    row_table,
):
    owners = lax.axis_size(EXPERT)
    tok, feature = pooled.shape
    hidden = in_weight.shape[1]
    half = hidden // lax.axis_size("dp")
    rows = ROWS * owners
    slots = 2 * BLOCKS * rows
    in_matrix, out_matrix = in_weight[0], out_weight[0]
    gate_flat = gate_weight.reshape(-1, feature)
    routes_t = routes.T
    in_vmem = pl.BlockSpec(memory_space=pltpu.VMEM)
    in_hbm = pl.BlockSpec(memory_space=pltpu.HBM)
    outbound = call(
        dispatch_kernel,
        jax.ShapeDtypeStruct((rows, BLOCKS * feature), BF),
        (far(routes_t), far(pooled)),
        1 << 27,
        "dispatch",
        4,
        in_specs=[in_hbm, in_hbm],
        out_specs=in_vmem,
        scratch_shapes=[
            pltpu.VMEM(routes_t.shape, jnp.int32),
            pltpu.VMEM(pooled.shape, BF),
            pltpu.SemaphoreType.DMA((2,)),
        ],
    )
    received = exchanged(outbound, ROWS)
    tall = 8 * owners
    take, put, gate_rows, lanes, side, bag_pick, bag_scale = call(
        prepare_kernel,
        shapes(
            ((2 * BLOCKS, tok, rows), BF),
            ((2 * SLOTS, owners, tok), BF),
            ((2, tok, feature), F32),
            ((2, tok, 128), F32),
            ((owners, 128), F32),
            ((tall, tok), BF),
            ((tall, 128), F32),
        ),
        (
            routes,
            routes_t,
            pooled,
            gate_flat,
            labels,
            bag_rows.reshape(owners, ENTRIES),
            bag_sample.reshape(owners, ENTRIES),
            bag_weight.reshape(owners, ENTRIES),
        ),
        1 << 31,
        "prepare",
        60,
    )
    depth = hidden // 2
    slopes = call(
        slope_kernel,
        jax.ShapeDtypeStruct((2, hidden), F32),
        (out_matrix, tower_weight),
        1 << 31,
        "slopes",
        60,
        grid=(hidden // depth,),
        in_specs=[pl.BlockSpec((depth, feature), lambda i: (i, 0)), full(tower_weight.shape)],
        out_specs=pl.BlockSpec((2, depth), lambda i: (0, i)),
    )
    message = call(
        expert_kernel,
        jax.ShapeDtypeStruct((rows, 3 * BLOCKS * feature), BF),
        (received, in_matrix, far(out_matrix), slopes, far(side)),
        7 << 30,
        "expert",
        40,
        in_specs=[in_vmem, in_vmem, in_hbm, in_vmem, pl.BlockSpec(memory_space=pl.ANY)],
        out_specs=in_vmem,
        scratch_shapes=[
            pltpu.VMEM((BLOCKS * rows, 3 * feature), F32),
            pltpu.VMEM((BLOCKS * rows, feature), BF),
            pltpu.VMEM((hidden, feature), BF),
            pltpu.SemaphoreType.DMA((hidden // CHUNK,)),
        ],
    )
    returned = exchanged(message, ROWS)
    received_other = swapped(received)
    tile = 512
    tiles = half // tile
    which = jnp.full((1,), lax.axis_index("dp"), jnp.int32)
    act_t, grad_t, slope = call(
        half_kernel,
        shapes(((half, slots), BF), ((half, slots), BF), ((half, 128), F32)),
        (which, received, received_other, in_matrix, out_matrix, tower_weight),
        7 << 30,
        "half",
        56,
        grid_spec=pltpu.PrefetchScalarGridSpec(
            num_scalar_prefetch=1,
            grid=(tiles,),
            in_specs=[
                full(received.shape),
                full(received.shape),
                pl.BlockSpec((tile, feature), lambda i, part: (part[0] * tiles + i, 0)),
                pl.BlockSpec((tile, feature), lambda i, part: (part[0] * tiles + i, 0)),
                full(tower_weight.shape),
            ],
            out_specs=[
                pl.BlockSpec((tile, slots), lambda i, part: (i, 0)),
                pl.BlockSpec((tile, slots), lambda i, part: (i, 0)),
                pl.BlockSpec((tile, 128), lambda i, part: (i, 0)),
            ],
        ),
    )
    sent = call(
        sample_kernel,
        jax.ShapeDtypeStruct((tall, feature), BF),
        (
            returned,
            take,
            far(put),
            far(gate_rows),
            far(lanes),
            far(side),
            far(bag_pick),
            far(bag_scale),
            tower_weight,
            tower_bias,
            far(slope),
        ),
        1 << 29,
        "sample",
        16,
        in_specs=[in_vmem] * 2 + [in_hbm] * 6 + [in_vmem]
        + [pl.BlockSpec(memory_space=pltpu.SMEM), pl.BlockSpec(memory_space=pl.ANY)],
        out_specs=in_vmem,
        scratch_shapes=[
            pltpu.VMEM(put.shape, BF),
            pltpu.VMEM(gate_rows.shape, F32),
            pltpu.VMEM(lanes.shape, F32),
            pltpu.VMEM(side.shape, F32),
            pltpu.VMEM(bag_pick.shape, BF),
            pltpu.VMEM(bag_scale.shape, F32),
            pltpu.SemaphoreType.DMA((6,)),
        ],
    )
    got = exchanged(sent, 8)
    got_other = swapped(got)
    table_tile = row_table.shape[0] // tiles
    in_grad, out_grad, gate_grad, tower_grad, new_table = call(
        final_kernel,
        shapes(
            ((half, feature), F32),
            ((half, feature), F32),
            ((2, feature), F32),
            ((2, feature), F32),
            (row_table.shape, F32),
        ),
        (received, received_other, got, got_other, far(act_t), far(grad_t), slope, tower_weight, row_table),
        6 << 30,
        "final",
        40,
        grid=(tiles,),
        in_specs=[
            full(received.shape),
            full(received.shape),
            full(got.shape),
            full(got.shape),
            in_hbm,
            in_hbm,
            pl.BlockSpec((tile, 128), lambda i: (i, 0)),
            full(tower_weight.shape),
            pl.BlockSpec((table_tile, feature), lambda i: (i, 0)),
        ],
        out_specs=[
            pl.BlockSpec((tile, feature), lambda i: (i, 0)),
            pl.BlockSpec((tile, feature), lambda i: (i, 0)),
            full((2, feature)),
            full((2, feature)),
            pl.BlockSpec((table_tile, feature), lambda i: (i, 0)),
        ],
        scratch_shapes=[
            pltpu.VMEM((slots, 2 * feature), BF),
            pltpu.VMEM((slots, feature), BF),
            pltpu.VMEM((16, tall), F32),
            pltpu.VMEM((half, slots), BF),
            pltpu.VMEM((half, slots), BF),
            pltpu.SemaphoreType.DMA((2, tiles)),
        ],
    )
    return (in_grad[None], out_grad[None], gate_grad[None], tower_grad, new_table)


def solution(mesh):
    split = Mesh(
        mesh.devices.reshape(4, 8, 4, mesh.shape["dp"]), ("expert_0", "expert_1", "expert_2", "dp")
    )
    in_specs = (
        P(EXPERT_DP, None),
        P(EXPERT_DP, None),
        P(EXPERT_DP, None),
        P(EXPERT, None, None),
        P(EXPERT, None, None),
        P(),
        P(),
        P(),
        P(EXPERT_DP),
        P(EXPERT_DP),
        P(EXPERT_DP),
        P(EXPERT, None),
    )
    out_specs = (
        P(EXPERT, "dp", None),
        P(EXPERT, "dp", None),
        P(EXPERT, None, None),
        P(),
        P(EXPERT, None),
    )
    return jax.shard_map(
        on_device, mesh=split, in_specs=in_specs, out_specs=out_specs, check_vma=False
    )
```

time: 158 us -> 135 us (0.85)
  waiting for transfers between devices: 34.3 us -> 23.4 us
  Pallas kernels: 48.8 us -> 40.9 us
  starting transfers between devices: 25.5 us -> 32.7 us
  blocking collectives: 31 us -> 24.6 us
  local copies, waits for them, and re-layouts: 16.1 us -> 12.3 us
    all_to_all x2, waiting for transfers between devices: 34.3 us -> 20.5 us  [exchanged(): lax.all_to_all(rows.reshape(-1, each, width), EXPERT, split_axis=0, conca...]
    all_to_all x2, starting transfers between devices: 17.3 us -> 26.2 us  [exchanged(): lax.all_to_all(rows.reshape(-1, each, width), EXPERT, split_axis=0, conca...]
    pallas_call x6 -> x7, Pallas kernels: 48.8 us -> 40.9 us  [call(): pl.pallas_call(kernel, out_shape=out_shape, cost_estimate=pl.CostEstimate...]
    all_to_all x1, blocking collectives: 31 us -> 24.6 us  [exchanged(): lax.all_to_all(rows.reshape(-1, each, width), EXPERT, split_axis=0, conca...]
    reshape x6 -> x5, local copies, waits for them, and re-layouts: 9.77 us -> 4.37 us  [the longest x2 2.18 us: exchanged(): rows.reshape(-1, each, width)]
    ppermute x2, waiting for transfers between devices: 0.01 us -> 2.89 us  [swapped(): return lax.ppermute(shard, 'dp', [(0, 1), (1, 0)])]
    ppermute x2, starting transfers between devices: 8.2 us -> 6.55 us  [swapped(): return lax.ppermute(shard, 'dp', [(0, 1), (1, 0)])]
    unnamed x22 -> x36, local copies, waits for them, and re-layouts: 3.22 us -> 4.13 us
  transfers between devices with their start and end apart: 4 -> 4, of which waited for: 2 -> 4; matrix products, arithmetic and copies ran while one was open for 3% -> 3% of each run, Pallas kernels for 9% -> 11%
where the time goes in v1:
time: 135 us
  Pallas kernels  40.9 us (30%)
  starting transfers between devices  32.7 us (24%)
  blocking collectives  24.6 us (18%)
  waiting for transfers between devices  23.4 us (17%)
  local copies, waits for them, and re-layouts  12.3 us (9%)
    pallas_call x7, Pallas kernels, call(): pl.pallas_call(kernel, out_shape=out_shape, cost_estimate=pl.CostEstimate...  40.9 us
    all_to_all x2, starting transfers between devices, exchanged(): lax.all_to_all(rows.reshape(-1, each, width), EXPERT, split_axis=0, conca...  26.2 us
    all_to_all x1, blocking collectives, exchanged(): lax.all_to_all(rows.reshape(-1, each, width), EXPERT, split_axis=0, conca...  24.6 us
    all_to_all x2, waiting for transfers between devices, exchanged(): lax.all_to_all(rows.reshape(-1, each, width), EXPERT, split_axis=0, conca...  20.5 us
    ppermute x2, starting transfers between devices, swapped(): return lax.ppermute(shard, 'dp', [(0, 1), (1, 0)])  6.55 us
    unnamed x36, local copies, waits for them, and re-layouts  4.13 us
    reshape x2, local copies, waits for them, and re-layouts, exchanged(): return moved.reshape(-1, width)  3.05 us
    ppermute x2, waiting for transfers between devices, swapped(): return lax.ppermute(shard, 'dp', [(0, 1), (1, 0)])  2.89 us
  transfers between devices with their start and end apart: 4, of which 4 were waited for; matrix products, arithmetic and copies ran while one was open for 3% of the time, Pallas kernels for 11%

profile of v1, /device:TPU:1, one launch (start us, length us, event | category | flops | bytes accessed | tf_op | source)
XLA Modules:
  0.0 134.9 jit_solution(388270294453853581)
XLA Ops:
  0.6 0.0 copy-start.12
  0.7 1.3 dispatch.1
  2.0 0.9 reshape.40
  2.9 16.5 %all-to-all-start = ((bf16[128,2,768]{2,1,0:T(2,128)(2,1)}), bf16[128,2,768]{2,1,0:T(2,128)(2,1)S(1)}, u32[]{:S(2)}, u32[]{:S(2)}) async-start(bf16[128,2,768]{2,1,0:T(2,128)(2,1)} %reshape.40), calls=%async_computation | async-start | bytes 786432 | tf_op jit(solution)/shard_map/all_to_all | solution.py:406
  19.4 0.8 copy.19.routes
  20.2 0.7 reshape.43.bag_rows
  21.0 0.7 reshape.44.bag_sample
  21.7 0.7 reshape.45.bag_weight
  22.4 0.8 copy.20.labels
  23.3 0.7 reshape.42.gate_flat
  24.0 2.6 %slopes.1 = f32[2,4096]{1,0:T(2,128)} custom-call(bf16[4096,256]{1,0:T(8,128)(2,1)} %bitcast.16, f32[2,256]{1,0:T(2,128)} %tower.7), custom_call_target="tpu_custom_call" | custom-call | flops 2147483648 | bytes 1048576 | tf_op jit(solution)/shard_map/slopes/pallas_call | solution.py:76
  26.6 3.6 %prepare.1 = (bf16[6,256,256]{2,1,0:T(8,128)(2,1)}, bf16[12,128,256]{2,1,0:T(8,128)(2,1)}, f32[2,256,256]{2,1,0:T(8,128)}, f32[2,256,128]{2,1,0:T(8,128)}, f32[1...) custom-call(s32[256,2]{1,0:T(8,128)} %copy.19.routes, s32[2,256]{1,0:T(2,128)} %bitcast.15, ...), custom_call_target="tpu_custom_call" | custom-call | flops 2147483648 | bytes 1048576 | tf_op jit(solution)/shard_map/prepare/pallas_call | solution.py:76
  30.2 3.9 %all-to-all-done = bf16[128,2,768]{2,1,0:T(2,128)(2,1)S(1)} async-done(((bf16[128,2,768]{2,1,0:T(2,128)(2,1)}), bf16[128,2,768]{2,1,0:T(2,128)(2,1)S(1)}, u32[]{:S(2)}, u32[]{:S(2)}) %all-to-all-start) | async-done | bytes 393248 | tf_op jit(solution)/shard_map/all_to_all | solution.py:406
  34.1 0.1 reshape.41.x
  34.2 0.0 copy-start.6
  34.3 1.7 %copy-done.6 = bf16[1,4096,256]{2,1,0:T(8,128)(2,1)S(1)} copy-done((bf16[1,4096,256]{2,1,0:T(8,128)(2,1)S(1)}, bf16[1,4096,256]{2,1,0:T(8,128)(2,1)}, u32[]{:S(2)}) %copy-start.6) | copy-done | bytes 2097176
  36.0 9.6 %expert.1 = bf16[256,2304]{1,0:T(8,128)(2,1)S(1)} custom-call(bf16[256,768]{1,0:T(8,128)(2,1)S(1)} %reshape.41.x, bf16[4096,256]{1,0:T(8,128)(2,1)S(1)} %bitcast.13, bf16[4096,256]{1,0:T(8,128)(2,1)} %bitcast.17, f32[2,4096]{1,0:T(2,128)S(1)} %copy-done.10, f32[128,128]{1,0:T(8,128)} %get-tuple-element.20.after.side_far), custom_call_target="tpu_custom_call" | custom-call | flops 7516192768 | bytes 1048576 | tf_op jit(solution)/shard_map/expert/pallas_call | solution.py:76
  45.6 1.3 reshape.46
  46.9 9.7 %all-to-all-start.1 = ((bf16[128,2,2304]{2,1,0:T(2,128)(2,1)}), bf16[128,2,2304]{2,1,0:T(2,128)(2,1)}, u32[]{:S(2)}, u32[]{:S(2)}) async-start(bf16[128,2,2304]{2,1,0:T(2,128)(2,1)} %reshape.46), calls=%async_computation.1 | async-start | bytes 2359296 | tf_op jit(solution)/shard_map/all_to_all | solution.py:406
  56.6 1.6 %collective-permute-start = (bf16[256,768]{1,0:T(8,128)(2,1)S(1)}, bf16[256,768]{1,0:T(8,128)(2,1)S(1)}, u32[]{:S(2)}, u32[]{:S(2)}) collective-permute-start(bf16[256,768]{1,0:T(8,128)(2,1)S(1)} %reshape.41.x), channel_id=1, source_target_pairs={{0,1},{1,0},{2,3},{3,2},{4,5},{5,4},{6,7},{7,6},{8,9},{9,8},{10,11... | collective-permute-start | bytes 1179656 | tf_op jit(solution)/shard_map/ppermute | solution.py:411
  58.2 1.3 %collective-permute-done.x_other = bf16[256,768]{1,0:T(8,128)(2,1)S(1)} collective-permute-done((bf16[256,768]{1,0:T(8,128)(2,1)S(1)}, bf16[256,768]{1,0:T(8,128)(2,1)S(1)}, u32[]{:S(2)}, u32[]{:S(2)}) %collective-permute-start) | collective-permute-done | bytes 393248 | tf_op jit(solution)/shard_map/ppermute | solution.py:411
  59.5 0.7 copy-done.8
  60.2 8.6 %half.1 = (bf16[2048,1536]{1,0:T(8,128)(2,1)}, bf16[2048,1536]{1,0:T(8,128)(2,1)}, f32[2048,128]{1,0:T(8,128)}) custom-call(s32[1]{0:T(128)} %bitcast.3.half, bf16[256,768]{1,0:T(8,128)(2,1)} %copy-done.2, bf16[256,768]{1,0:T(8,128)(2,1)} %copy-done.8, bf16[4096,256]{1,0:T(8,128)(2,1)} %bitcast.12, bf16[4096,256]{1,0:T(8,128)(2,1)} %bitcast.18, f32[2,256]{1,0:T(2,128)} %tower.7), custom_call_target="tpu_custom_call" | custom-call | flops 7516192768 | bytes 1048576 | tf_op jit(solution)/shard_map/half/pallas_call | solution.py:76
  68.9 0.0 copy-start.5
  68.9 16.6 %all-to-all-done.1 = bf16[128,2,2304]{2,1,0:T(2,128)(2,1)} async-done(((bf16[128,2,2304]{2,1,0:T(2,128)(2,1)}), bf16[128,2,2304]{2,1,0:T(2,128)(2,1)}, u32[]{:S(2)}, u32[]{:S(2)}) %all-to-all-start.1) | async-done | bytes 1179680 | tf_op jit(solution)/shard_map/all_to_all | solution.py:406
  85.5 2.9 %reshape.47.back = bf16[256,2304]{1,0:T(8,128)(2,1)S(1)} reshape(bf16[128,2,2304]{2,1,0:T(2,128)(2,1)} %all-to-all-done.1) | data formatting | bytes 2359296 | tf_op jit(solution)/shard_map/reshape | solution.py:407
  88.5 0.0 copy-start
  88.5 4.5 %sample.1 = bf16[1024,256]{1,0:T(8,128)(2,1)S(1)} custom-call(bf16[256,2304]{1,0:T(8,128)(2,1)S(1)} %reshape.47.back, bf16[6,256,256]{2,1,0:T(8,128)(2,1)S(1)} %copy-done.1, bf16[12,128,256]{2,1,0:T(8,128)(2,1)} %get-tuple-element.22.put_far, f32[2,256,256]{2,1,0:T(8,128)} %get-tuple-element.23.gate_rows_far, f32[2,256,128]{2,1,0:T(8,128)} %get-tuple-element.24.lanes_far, ...), custom_call_target="tpu_custom_call" | custom-call | flops 536870912 | bytes 1048576 | tf_op jit(solution)/shard_map/sample/pallas_call | solution.py:76
  93.0 24.6 %all_to_all.15 = bf16[128,8,256]{2,1,0:T(8,128)(2,1)S(1)} all-to-all(bf16[128,8,256]{2,1,0:T(8,128)(2,1)S(1)} %bitcast.9), channel_id=1, replica_groups=mesh['expert_0'=4,'expert_1'=8,'expert_2'=4,'dp'=2] {'expert_0','expert_..., dimensions={0} | all-to-all | bytes 1048576 | tf_op jit(solution)/shard_map/all_to_all | solution.py:406
  117.6 5.0 %collective-permute-start.1 = (bf16[1024,256]{1,0:T(8,128)(2,1)S(1)}, bf16[1024,256]{1,0:T(8,128)(2,1)S(1)}, u32[]{:S(2)}, u32[]{:S(2)}) collective-permute-start(bf16[1024,256]{1,0:T(8,128)(2,1)S(1)} %bitcast.10), channel_id=1, source_target_pairs={{0,1},{1,0},{2,3},{3,2},{4,5},{5,4},{6,7},{7,6},{8,9},{9,8},{10,11... | collective-permute-start | bytes 1572872 | tf_op jit(solution)/shard_map/ppermute | solution.py:411
  122.6 1.5 %collective-permute-done.1.got_other = bf16[1024,256]{1,0:T(8,128)(2,1)S(1)} collective-permute-done((bf16[1024,256]{1,0:T(8,128)(2,1)S(1)}, bf16[1024,256]{1,0:T(8,128)(2,1)S(1)}, u32[]{:S(2)}, u32[]{:S(2)}) %collective-permute-start.1) | collective-permute-done | bytes 524320 | tf_op jit(solution)/shard_map/ppermute | solution.py:411
  124.1 10.6 %final.1 = (f32[2048,256]{1,0:T(8,128)}, f32[2048,256]{1,0:T(8,128)}, f32[2,256]{1,0:T(2,128)}, f32[2,256]{1,0:T(2,128)}, f32[1024,256]{1,0:T(8,128)}) custom-call(bf16[256,768]{1,0:T(8,128)(2,1)S(1)} %copy-done.3, bf16[256,768]{1,0:T(8,128)(2,1)S(1)} %copy-done.9, bf16[1024,256]{1,0:T(8,128)(2,1)S(1)} %bitcast.11, ...), custom_call_target="tpu_custom_call" | custom-call | flops 6442450944 | bytes 1048576 | tf_op jit(solution)/shard_map/final/pallas_call | solution.py:76
  (28 shorter events, 0.1 us)
Async XLA Ops:
  0.6 18.8 %copy-start.12 = (s32[256,2]{0,1:T(2,128)S(1)}, s32[256,2]{0,1:T(2,128)}, u32[]{:S(2)}) copy-start(s32[256,2]{0,1:T(2,128)} %param.13) | copy-start | bytes 6148
  0.6 19.6 %copy-start.14 = (s32[512]{0:T(512)S(1)}, s32[512]{0:T(512)}, u32[]{:S(2)}) copy-start(s32[512]{0:T(512)} %param.20) | copy-start | bytes 6148
  0.7 20.3 %copy-start.15 = (s32[512]{0:T(512)S(1)}, s32[512]{0:T(512)}, u32[]{:S(2)}) copy-start(s32[512]{0:T(512)} %param.21) | copy-start | bytes 6148
  0.7 21.0 %copy-start.16 = (f32[512]{0:T(512)S(1)}, f32[512]{0:T(512)}, u32[]{:S(2)}) copy-start(f32[512]{0:T(512)} %param.22) | copy-start | bytes 6148
  0.7 21.8 %copy-start.13 = (s32[256,2]{0,1:T(2,128)S(1)}, s32[256,2]{0,1:T(2,128)}, u32[]{:S(2)}) copy-start(s32[256,2]{0,1:T(2,128)} %param.14) | copy-start | bytes 6148
  0.7 22.6 %copy-start.11 = (bf16[128,2,256]{2,1,0:T(2,128)(2,1)S(1)}, bf16[128,2,256]{2,1,0:T(2,128)(2,1)}, u32[]{:S(2)}) copy-start(bf16[128,2,256]{2,1,0:T(2,128)(2,1)} %param.17) | copy-start | bytes 393220
  2.9 31.2 %all-to-all-start = ((bf16[128,2,768]{2,1,0:T(2,128)(2,1)}), bf16[128,2,768]{2,1,0:T(2,128)(2,1)S(1)}, u32[]{:S(2)}, u32[]{:S(2)}) async-start(bf16[128,2,768]{2,1,0:T(2,128)(2,1)} %reshape.40), calls=%async_computation | async-start | bytes 786432 | tf_op jit(solution)/shard_map/all_to_all | solution.py:406
  26.6 7.7 %copy-start.10 = (f32[2,4096]{1,0:T(2,128)S(1)}, f32[2,4096]{1,0:T(2,128)}, u32[]{:S(2)}) copy-start(f32[2,4096]{1,0:T(2,128)} %slopes.1) | copy-start | bytes 98308
  34.2 22.3 %copy-start.2 = (bf16[256,768]{1,0:T(8,128)(2,1)}, bf16[256,768]{1,0:T(8,128)(2,1)S(1)}, u32[]{:S(2)}) copy-start(bf16[256,768]{1,0:T(8,128)(2,1)S(1)} %reshape.41.x) | copy-start | bytes 1179652
  34.2 1.7 %copy-start.6 = (bf16[1,4096,256]{2,1,0:T(8,128)(2,1)S(1)}, bf16[1,4096,256]{2,1,0:T(8,128)(2,1)}, u32[]{:S(2)}) copy-start(bf16[1,4096,256]{2,1,0:T(8,128)(2,1)} %param.15) | copy-start | bytes 6291460
  46.9 38.6 %all-to-all-start.1 = ((bf16[128,2,2304]{2,1,0:T(2,128)(2,1)}), bf16[128,2,2304]{2,1,0:T(2,128)(2,1)}, u32[]{:S(2)}, u32[]{:S(2)}) async-start(bf16[128,2,2304]{2,1,0:T(2,128)(2,1)} %reshape.46), calls=%async_computation.1 | async-start | bytes 2359296 | tf_op jit(solution)/shard_map/all_to_all | solution.py:406
  56.6 3.0 %collective-permute-start = (bf16[256,768]{1,0:T(8,128)(2,1)S(1)}, bf16[256,768]{1,0:T(8,128)(2,1)S(1)}, u32[]{:S(2)}, u32[]{:S(2)}) collective-permute-start(bf16[256,768]{1,0:T(8,128)(2,1)S(1)} %reshape.41.x), channel_id=1, source_target_pairs={{0,1},{1,0},{2,3},{3,2},{4,5},{5,4},{6,7},{7,6},{8,9},{9,8},{10,11... | collective-permute-start | bytes 1179656 | tf_op jit(solution)/shard_map/ppermute | solution.py:411
  59.5 0.7 copy-start.8
  68.9 19.6 %copy-start.1 = (bf16[6,256,256]{2,1,0:T(8,128)(2,1)S(1)}, bf16[6,256,256]{2,1,0:T(8,128)(2,1)}, u32[]{:S(2)}) copy-start(bf16[6,256,256]{2,1,0:T(8,128)(2,1)} %get-tuple-element.21.take) | copy-start | bytes 2359300
  68.9 19.6 %copy-start.4 = (f32[2,256]{1,0:T(2,128)S(1)}, f32[2,256]{1,0:T(2,128)}, u32[]{:S(2)}) copy-start(f32[2,256]{1,0:T(2,128)} %tower.7) | copy-start | bytes 6148
  68.9 19.6 %copy-start.5 = (f32[2]{0:T(128)S(1)}, f32[2]{0:T(128)}, u32[]{:S(2)}) copy-start(f32[2]{0:T(128)} %bias.1) | copy-start | bytes 28
  88.5 35.7 %copy-start = (f32[2048,128]{1,0:T(8,128)S(1)}, f32[2048,128]{1,0:T(8,128)}, u32[]{:S(2)}) copy-start(f32[2048,128]{1,0:T(8,128)} %get-tuple-element.27.after.slope) | copy-start | bytes 3145732
  88.5 35.7 %copy-start.3 = (bf16[256,768]{1,0:T(8,128)(2,1)S(1)}, bf16[256,768]{1,0:T(8,128)(2,1)}, u32[]{:S(2)}) copy-start(bf16[256,768]{1,0:T(8,128)(2,1)} %copy-done.2) | copy-start | bytes 1179652
  88.5 35.7 %copy-start.7 = (f32[1024,256]{1,0:T(8,128)S(1)}, f32[1024,256]{1,0:T(8,128)}, u32[]{:S(2)}) copy-start(f32[1024,256]{1,0:T(8,128)} %table.1) | copy-start | bytes 3145732
  88.5 35.6 %copy-start.9 = (bf16[256,768]{1,0:T(8,128)(2,1)S(1)}, bf16[256,768]{1,0:T(8,128)(2,1)}, u32[]{:S(2)}) copy-start(bf16[256,768]{1,0:T(8,128)(2,1)} %copy-done.8) | copy-start | bytes 1179652
  117.6 6.5 %collective-permute-start.1 = (bf16[1024,256]{1,0:T(8,128)(2,1)S(1)}, bf16[1024,256]{1,0:T(8,128)(2,1)S(1)}, u32[]{:S(2)}, u32[]{:S(2)}) collective-permute-start(bf16[1024,256]{1,0:T(8,128)(2,1)S(1)} %bitcast.10), channel_id=1, source_target_pairs={{0,1},{1,0},{2,3},{3,2},{4,5},{5,4},{6,7},{7,6},{8,9},{9,8},{10,11... | collective-permute-start | bytes 1572872 | tf_op jit(solution)/shard_map/ppermute | solution.py:411

commit v2 on v1

--- a/solution.py
+++ b/solution.py
@@ -171,8 +171,7 @@
         slopes[t : t + 1, :] = found[t : t + 1] + found[2 + t : 3 + t] + found[4 + t : 5 + t]
 
 
-def expert_kernel(x, w_in, w_out_far, slopes, after, out, total, stacked, w_out, sems):
-    del after
+def expert_kernel(x, w_in, w_out_far, slopes, out, total, stacked, w_out, sems):
     rows = x.shape[0]
     hidden, feature = w_out.shape
     wide = 3 * feature
@@ -223,12 +222,13 @@
 
 
 def sample_kernel(
-    back, take, put_far, gate_rows_far, lanes_far, side_far, bag_pick_far, bag_scale_far,
+    back, take_far, put_far, gate_rows_far, lanes_far, side_far, bag_pick_far, bag_scale_far,
     tower, bias, after,
-    out, put, gate_rows, lanes, side, bag_pick, bag_scale, sems,
+    out, take, put, gate_rows, lanes, side, bag_pick, bag_scale, sems,
 ):
     del after
     pairs = (
+        (take_far, take),
         (lanes_far, lanes),
         (gate_rows_far, gate_rows),
         (bag_pick_far, bag_pick),
@@ -242,6 +242,7 @@
     feature = tower.shape[1]
     wide = 3 * feature
     parts = []
+    copies[0].wait()
     for k in range(2):
         part = dot(take[BLOCKS * k], back[:, :wide])
         for c in range(1, BLOCKS):
@@ -256,7 +257,7 @@
     for k in range(2):
         result = parts[k][:, :feature].astype(BF)
         along.append(sum(dot_last(result, weight) for weight in weights))
-    for copy in copies:
+    for copy in copies[1:]:
         copy.wait()
     first, label = lanes[0], lanes[1]
     second = 1.0 - first
@@ -302,31 +303,67 @@
         out[:, cols] = (value + extra if at == 0 else value).astype(BF)
 
 
+def decode(inputs, source, tower, scaled, routed):
+    feature = tower.shape[1]
+    rows, tall = inputs.shape[0], source.shape[0]
+    row = iota((rows, tall), 0)
+    expand = ones_where(iota((rows, tall), 1) == 8 * (row >> 1) + SIDE_ROW)
+    lane = iota((rows, 128), 1)
+    half_lanes = BLOCKS * SLOT_LANES
+    odd = (iota((rows, 128), 0) & 1) == 1
+    own = (odd & (lane >= half_lanes) & (lane < ROW_LANES)) | (~odd & (lane < half_lanes))
+    source_lane = iota((128, feature), 0)
+    within = jnp.where(source_lane >= half_lanes, source_lane - half_lanes, source_lane)
+    side = jnp.where(own, dot(expand, source[:, :128]), 0.0).astype(BF)
+    gate_total = [jnp.zeros((1, feature), F32) for _ in range(2)]
+    for c in range(BLOCKS):
+        values = []
+        for v in range(4):
+            base = c * SLOT_LANES + 2 * PIECES * (v // 2) + v % 2
+            values.append(dot(side, ones_where((within == base) | (within == base + 2) | (within == base + 4))))
+        block = inputs[:, c * feature : (c + 1) * feature].astype(F32)
+        at = slice(c * rows, (c + 1) * rows)
+        routed[at, :] = (values[0] * tower[0:1, :] + values[1] * tower[1:2, :]).astype(BF)
+        for t in range(2):
+            scaled[at, t * feature : (t + 1) * feature] = (values[t] * block).astype(BF)
+            gate_total[t] += jnp.sum(values[2 + t] * block, axis=0, keepdims=True)
+    tower_pick = ones_where((iota((8, tall), 1) & 7) == TOWER_ROW + iota((8, tall), 0))
+    tower_total = dot(tower_pick, source[...])
+    wanted, asked = iota((8, 128), 1), iota((8, 128), 0)
+    select = jnp.where(wanted == ROW_LANES + 2 * asked, 256.0, 0.0)
+    select = jnp.where(wanted == ROW_LANES + 2 * asked + 1, 1.0, select).astype(BF)
+    numbers = dot_last(select, source[:, :128])
+    which = iota((1, tall), 1) & 7
+    target = jnp.full((1, tall), -1.0, F32)
+    for e in range(ENTRIES):
+        moved = pltpu.roll(numbers, tall + e - SIDE_ROW, 1)
+        target = jnp.where(which == e, moved[e : e + 1], target)
+    return gate_total, tower_total, target
+
+
+def row_sums(target, source, start, depth):
+    number = (start + iota((depth, source.shape[0]), 0)).astype(F32)
+    return dot(ones_where(number == target), source[...])
+
+
+def own_kernel(x, got, tower, table, scaled, routed, gate_part, tower_part, table_part):
+    gate_total, tower_total, target = decode(x, got, tower, scaled, routed)
+    for t in range(2):
+        gate_part[t : t + 1, :] = gate_total[t]
+        tower_part[t : t + 1, :] = tower_total[t : t + 1]
+    depth = 256
+    for start in range(0, table.shape[0], depth):
+        at = slice(start, start + depth)
+        table_part[at, :] = table[at, :] - STEP_SIZE * row_sums(target, got, start, depth)
+
+
 def final_kernel(
-    x,
-    x_other,
-    got,
-    got_other,
-    act_far,
-    grad_far,
-    slope,
-    tower,
-    table,
-    in_grad,
-    out_grad,
-    gate_grad,
-    tower_grad,
-    new_table,
-    scaled,
-    routed,
-    targets,
-    act_t,
-    grad_t,
-    sems,
+    x_other, got_other, scaled_own, routed_own, act_far, grad_far, slope, tower,
+    gate_part, tower_part, table_part,
+    in_grad, out_grad, gate_grad, tower_grad, new_table,
+    scaled, routed, targets, act_t, grad_t, sems,
 ):
     feature = tower.shape[1]
-    rows = x.shape[0]
-    tall = got.shape[0]
     step = pl.program_id(0)
     tile = in_grad.shape[0]
 
@@ -334,8 +371,8 @@
         part = pl.ds(n * tile, tile)
         pairs = ((grad_far, grad_t), (act_far, act_t))
         return [
-            pltpu.make_async_copy(far.at[part, :], near.at[part, :], sems.at[m, n])
-            for m, (far, near) in enumerate(pairs)
+            pltpu.make_async_copy(distant.at[part, :], near.at[part, :], sems.at[m, n])
+            for m, (distant, near) in enumerate(pairs)
         ]
 
     @pl.when(step == 0)
@@ -343,62 +380,22 @@
         for n in range(act_t.shape[0] // tile):
             for copy in arriving(n):
                 copy.start()
-        gate_total = [jnp.zeros((1, feature), F32) for _ in range(2)]
-        tower_total = jnp.zeros((8, feature), F32)
-        row = iota((rows, tall), 0)
-        expand = ones_where(iota((rows, tall), 1) == 8 * (row >> 1) + SIDE_ROW)
-        lane = iota((rows, 128), 1)
-        half_lanes = BLOCKS * SLOT_LANES
-        odd = (iota((rows, 128), 0) & 1) == 1
-        own = (odd & (lane >= half_lanes) & (lane < ROW_LANES)) | (~odd & (lane < half_lanes))
-        source_lane = iota((128, feature), 0)
-        within = jnp.where(source_lane >= half_lanes, source_lane - half_lanes, source_lane)
-        gather = {}
-        for c in range(BLOCKS):
-            for v in range(4):
-                base = c * SLOT_LANES + 2 * PIECES * (v // 2) + v % 2
-                gather[c, v] = ones_where((within == base) | (within == base + 2) | (within == base + 4))
-        wanted, asked = iota((8, 128), 1), iota((8, 128), 0)
-        select = jnp.where(wanted == ROW_LANES + 2 * asked, 256.0, 0.0)
-        select = jnp.where(wanted == ROW_LANES + 2 * asked + 1, 1.0, select).astype(BF)
-        which = iota((1, tall), 1) & 7
-        tower_pick = ones_where((iota((8, tall), 1) & 7) == TOWER_ROW + iota((8, tall), 0))
-        for r, (inputs, source) in enumerate(((x, got), (x_other, got_other))):
-            numbers = dot_last(select, source[:, :128])
-            target = jnp.full((1, tall), -1.0, F32)
-            for e in range(ENTRIES):
-                moved = pltpu.roll(numbers, tall + e - SIDE_ROW if e < SIDE_ROW else 0, 1)
-                target = jnp.where(which == e, moved[e : e + 1], target)
-            targets[8 * r : 8 * r + 8, :] = jnp.broadcast_to(target, (8, tall))
-            tower_total += dot(tower_pick, source[...])
-            side = jnp.where(own, dot(expand, source[:, :128]), 0.0).astype(BF)
-            for c in range(BLOCKS):
-                values = [dot(side, gather[c, v]) for v in range(4)]
-                at = (BLOCKS * r + c) * rows
-                block = inputs[:, c * feature : (c + 1) * feature].astype(F32)
-                routed[at : at + rows, :] = (
-                    values[0] * tower[0:1, :] + values[1] * tower[1:2, :]
-                ).astype(BF)
-                for t in range(2):
-                    cols = slice(t * feature, (t + 1) * feature)
-                    scaled[at : at + rows, cols] = (values[t] * block).astype(BF)
-                    gate_total[t] += jnp.sum(values[2 + t] * block, axis=0, keepdims=True)
+        gate_total, tower_total, target = decode(x_other, got_other, tower, scaled, routed)
+        targets[...] = jnp.broadcast_to(target, targets.shape)
         for t in range(2):
-            gate_grad[t : t + 1, :] = gate_total[t]
-            tower_grad[t : t + 1, :] = tower_total[t : t + 1]
+            gate_grad[t : t + 1, :] = gate_part[t : t + 1, :] + gate_total[t]
+            tower_grad[t : t + 1, :] = tower_part[t : t + 1, :] + tower_total[t : t + 1]
 
     for copy in arriving(step):
         copy.wait()
     part = pl.ds(pl.multiple_of(step * tile, tile), tile)
-    both = dot(grad_t[part, :], scaled[...])
+    split = scaled.shape[0]
+    both = dot(grad_t[part, :split], scaled_own[...]) + dot(grad_t[part, split:], scaled[...])
     in_grad[...] = slope[:, 0:1] * both[:, :feature] + slope[:, 1:2] * both[:, feature:]
-    out_grad[...] = dot(act_t[part, :], routed[...])
-    depth = table.shape[0]
-    number = (step * depth + iota((depth, tall), 0)).astype(F32)
-    sums = jnp.zeros(table.shape, F32)
-    for r, source in enumerate((got, got_other)):
-        sums += dot(ones_where(number == targets[8 * r : 8 * r + 1, :]), source[...])
-    new_table[...] = table[...] - STEP_SIZE * sums
+    out_grad[...] = dot(act_t[part, :split], routed_own[...]) + dot(act_t[part, split:], routed[...])
+    depth = new_table.shape[0]
+    sums = row_sums(targets[0:1, :], got_other, step * depth, depth)
+    new_table[...] = table_part[...] - STEP_SIZE * sums
 
 
 def exchanged(rows, each):
@@ -501,11 +498,11 @@
     message = call(
         expert_kernel,
         jax.ShapeDtypeStruct((rows, 3 * BLOCKS * feature), BF),
-        (received, in_matrix, far(out_matrix), slopes, far(side)),
+        (received, in_matrix, far(out_matrix), slopes),
         7 << 30,
         "expert",
         40,
-        in_specs=[in_vmem, in_vmem, in_hbm, in_vmem, pl.BlockSpec(memory_space=pl.ANY)],
+        in_specs=[in_vmem, in_vmem, in_hbm, in_vmem],
         out_specs=in_vmem,
         scratch_shapes=[
             pltpu.VMEM((BLOCKS * rows, 3 * feature), F32),
@@ -548,7 +545,7 @@
         jax.ShapeDtypeStruct((tall, feature), BF),
         (
             returned,
-            take,
+            far(take),
             far(put),
             far(gate_rows),
             far(lanes),
@@ -562,21 +559,37 @@
         1 << 29,
         "sample",
         16,
-        in_specs=[in_vmem] * 2 + [in_hbm] * 6 + [in_vmem]
+        in_specs=[in_vmem] + [in_hbm] * 7 + [in_vmem]
         + [pl.BlockSpec(memory_space=pltpu.SMEM), pl.BlockSpec(memory_space=pl.ANY)],
         out_specs=in_vmem,
         scratch_shapes=[
+            pltpu.VMEM(take.shape, BF),
             pltpu.VMEM(put.shape, BF),
             pltpu.VMEM(gate_rows.shape, F32),
             pltpu.VMEM(lanes.shape, F32),
             pltpu.VMEM(side.shape, F32),
             pltpu.VMEM(bag_pick.shape, BF),
             pltpu.VMEM(bag_scale.shape, F32),
-            pltpu.SemaphoreType.DMA((6,)),
+            pltpu.SemaphoreType.DMA((7,)),
         ],
     )
     got = exchanged(sent, 8)
     got_other = swapped(got)
+    own_slots = slots // 2
+    scaled, routed, gate_part, tower_part, table_part = call(
+        own_kernel,
+        shapes(
+            ((own_slots, 2 * feature), BF),
+            ((own_slots, feature), BF),
+            ((2, feature), F32),
+            ((2, feature), F32),
+            (row_table.shape, F32),
+        ),
+        (received, got, tower_weight, row_table),
+        1 << 29,
+        "own",
+        12,
+    )
     table_tile = row_table.shape[0] // tiles
     in_grad, out_grad, gate_grad, tower_grad, new_table = call(
         final_kernel,
@@ -587,20 +600,34 @@
             ((2, feature), F32),
             (row_table.shape, F32),
         ),
-        (received, received_other, got, got_other, far(act_t), far(grad_t), slope, tower_weight, row_table),
+        (
+            received_other,
+            got_other,
+            scaled,
+            routed,
+            far(act_t),
+            far(grad_t),
+            slope,
+            tower_weight,
+            gate_part,
+            tower_part,
+            table_part,
+        ),
         6 << 30,
         "final",
         40,
         grid=(tiles,),
         in_specs=[
             full(received.shape),
-            full(received.shape),
             full(got.shape),
-            full(got.shape),
+            full(scaled.shape),
+            full(routed.shape),
             in_hbm,
             in_hbm,
             pl.BlockSpec((tile, 128), lambda i: (i, 0)),
             full(tower_weight.shape),
+            full((2, feature)),
+            full((2, feature)),
             pl.BlockSpec((table_tile, feature), lambda i: (i, 0)),
         ],
         out_specs=[
@@ -611,9 +638,9 @@
             pl.BlockSpec((table_tile, feature), lambda i: (i, 0)),
         ],
         scratch_shapes=[
-            pltpu.VMEM((slots, 2 * feature), BF),
-            pltpu.VMEM((slots, feature), BF),
-            pltpu.VMEM((16, tall), F32),
+            pltpu.VMEM((own_slots, 2 * feature), BF),
+            pltpu.VMEM((own_slots, feature), BF),
+            pltpu.VMEM((8, tall), F32),
             pltpu.VMEM((half, slots), BF),
             pltpu.VMEM((half, slots), BF),
             pltpu.SemaphoreType.DMA((2, tiles)),

time: 135 us -> 131 us (0.970)
  waiting for transfers between devices: 23.4 us -> 21.6 us
  local copies, waits for them, and re-layouts: 12.3 us -> 10.6 us
    ppermute x2, waiting for transfers between devices: 2.89 us -> 0.01 us  [swapped(): return lax.ppermute(shard, 'dp', [(0, 1), (1, 0)])]
    reshape x2, local copies, waits for them, and re-layouts: 3.05 us -> 0.61 us  [exchanged(): return moved.reshape(-1, width)]
    all_to_all x2, starting transfers between devices: 26.2 us -> 24.2 us  [exchanged(): lax.all_to_all(rows.reshape(-1, each, width), EXPERT, split_axis=0, conca...]
    pallas_call x7 -> x8, Pallas kernels: 40.9 us -> 41.7 us  [call(): pl.pallas_call(kernel, out_shape=out_shape, cost_estimate=pl.CostEstimate...]
    unnamed x36 -> x34, local copies, waits for them, and re-layouts: 4.13 us -> 4.91 us
  transfers between devices with their start and end apart: 4 -> 4, of which waited for: 4 -> 2; matrix products, arithmetic and copies ran while one was open for 3% -> 3% of each run, Pallas kernels for 11% -> 13%
where the time goes in v2:
time: 131 us
  Pallas kernels  41.7 us (32%)
  starting transfers between devices  31.4 us (24%)
  blocking collectives  24.6 us (19%)
  waiting for transfers between devices  21.6 us (16%)
  local copies, waits for them, and re-layouts  10.6 us (8%)
    pallas_call x8, Pallas kernels, call(): pl.pallas_call(kernel, out_shape=out_shape, cost_estimate=pl.CostEstimate...  41.7 us
    all_to_all x1, blocking collectives, exchanged(): lax.all_to_all(rows.reshape(-1, each, width), EXPERT, split_axis=0, conca...  24.6 us
    all_to_all x2, starting transfers between devices, exchanged(): lax.all_to_all(rows.reshape(-1, each, width), EXPERT, split_axis=0, conca...  24.2 us
    all_to_all x2, waiting for transfers between devices, exchanged(): lax.all_to_all(rows.reshape(-1, each, width), EXPERT, split_axis=0, conca...  21.6 us
    ppermute x2, starting transfers between devices, swapped(): return lax.ppermute(shard, 'dp', [(0, 1), (1, 0)])  7.18 us
    unnamed x34, local copies, waits for them, and re-layouts  4.91 us
  transfers between devices with their start and end apart: 4, of which 2 were waited for; matrix products, arithmetic and copies ran while one was open for 3% of the time, Pallas kernels for 13%

profile of v2, /device:TPU:1, one launch (start us, length us, event | category | flops | bytes accessed | tf_op | source)
XLA Modules:
  0.0 130.9 jit_solution(10340588906296084288)
XLA Ops:
  0.6 1.3 dispatch.1
  1.9 0.9 reshape.40
  2.8 16.3 %all-to-all-start = ((bf16[128,2,768]{2,1,0:T(2,128)(2,1)}), bf16[128,2,768]{2,1,0:T(2,128)(2,1)S(1)}, u32[]{:S(2)}, u32[]{:S(2)}) async-start(bf16[128,2,768]{2,1,0:T(2,128)(2,1)} %reshape.40), calls=%async_computation | async-start | bytes 786432 | tf_op jit(solution)/shard_map/all_to_all | solution.py:403
  19.1 2.6 %slopes.1 = f32[2,4096]{1,0:T(2,128)} custom-call(bf16[4096,256]{1,0:T(8,128)(2,1)} %bitcast.16, f32[2,256]{1,0:T(2,128)} %tower.9), custom_call_target="tpu_custom_call" | custom-call | flops 2147483648 | bytes 1048576 | tf_op jit(solution)/shard_map/slopes/pallas_call | solution.py:76
  21.8 12.2 %all-to-all-done = bf16[128,2,768]{2,1,0:T(2,128)(2,1)S(1)} async-done(((bf16[128,2,768]{2,1,0:T(2,128)(2,1)}), bf16[128,2,768]{2,1,0:T(2,128)(2,1)S(1)}, u32[]{:S(2)}, u32[]{:S(2)}) %all-to-all-start) | async-done | bytes 393248 | tf_op jit(solution)/shard_map/all_to_all | solution.py:403
  34.0 0.1 reshape.41.x
  34.1 0.0 copy-start.5
  34.2 1.7 %copy-done.5 = bf16[1,4096,256]{2,1,0:T(8,128)(2,1)S(1)} copy-done((bf16[1,4096,256]{2,1,0:T(8,128)(2,1)S(1)}, bf16[1,4096,256]{2,1,0:T(8,128)(2,1)}, u32[]{:S(2)}) %copy-start.5) | copy-done | bytes 2097176
  35.9 0.8 copy-done.9
  36.6 9.6 %expert.1 = bf16[256,2304]{1,0:T(8,128)(2,1)S(1)} custom-call(bf16[256,768]{1,0:T(8,128)(2,1)S(1)} %reshape.41.x, bf16[4096,256]{1,0:T(8,128)(2,1)S(1)} %bitcast.13, bf16[4096,256]{1,0:T(8,128)(2,1)} %bitcast.17, f32[2,4096]{1,0:T(2,128)S(1)} %copy-done.9), custom_call_target="tpu_custom_call" | custom-call | flops 7516192768 | bytes 1048576 | tf_op jit(solution)/shard_map/expert/pallas_call | solution.py:76
  46.3 0.0 copy-start.13
  46.3 0.0 copy-start.14
  46.3 0.0 copy-start.10
  46.3 1.3 reshape.42
  47.6 7.8 %all-to-all-start.1 = ((bf16[128,2,2304]{2,1,0:T(2,128)(2,1)}), bf16[128,2,2304]{2,1,0:T(2,128)(2,1)S(1)}, u32[]{:S(2)}, u32[]{:S(2)}) async-start(bf16[128,2,2304]{2,1,0:T(2,128)(2,1)} %reshape.42), calls=%async_computation.1 | async-start | bytes 2359296 | tf_op jit(solution)/shard_map/all_to_all | solution.py:403
  55.5 2.1 %collective-permute-start = (bf16[256,768]{1,0:T(8,128)(2,1)S(1)}, bf16[256,768]{1,0:T(8,128)(2,1)S(1)}, u32[]{:S(2)}, u32[]{:S(2)}) collective-permute-start(bf16[256,768]{1,0:T(8,128)(2,1)S(1)} %reshape.41.x), channel_id=1, source_target_pairs={{0,1},{1,0},{2,3},{3,2},{4,5},{5,4},{6,7},{7,6},{8,9},{9,8},{10,11... | collective-permute-start | bytes 1179656 | tf_op jit(solution)/shard_map/ppermute | solution.py:408
  57.6 0.8 copy.19.routes
  58.4 0.7 reshape.45.bag_rows
  59.1 0.7 reshape.46.bag_sample
  59.8 0.7 reshape.47.bag_weight
  60.6 0.8 copy.20.labels
  61.4 0.7 reshape.44.gate_flat
  62.1 3.6 %prepare.1 = (bf16[6,256,256]{2,1,0:T(8,128)(2,1)}, bf16[12,128,256]{2,1,0:T(8,128)(2,1)}, f32[2,256,256]{2,1,0:T(8,128)}, f32[2,256,128]{2,1,0:T(8,128)}, f32[1...) custom-call(s32[256,2]{1,0:T(8,128)} %copy.19.routes, s32[2,256]{1,0:T(2,128)} %bitcast.15, ...), custom_call_target="tpu_custom_call" | custom-call | flops 2147483648 | bytes 1048576 | tf_op jit(solution)/shard_map/prepare/pallas_call | solution.py:76
  65.7 0.8 copy-done.7
  66.4 8.6 %half.1 = (bf16[2048,1536]{1,0:T(8,128)(2,1)}, bf16[2048,1536]{1,0:T(8,128)(2,1)}, f32[2048,128]{1,0:T(8,128)}) custom-call(s32[1]{0:T(128)} %bitcast.3.half, bf16[256,768]{1,0:T(8,128)(2,1)} %copy-done.1, bf16[256,768]{1,0:T(8,128)(2,1)} %copy-done.7, bf16[4096,256]{1,0:T(8,128)(2,1)} %bitcast.12, bf16[4096,256]{1,0:T(8,128)(2,1)} %bitcast.18, f32[2,256]{1,0:T(2,128)} %tower.9), custom_call_target="tpu_custom_call" | custom-call | flops 7516192768 | bytes 1048576 | tf_op jit(solution)/shard_map/half/pallas_call | solution.py:76
  75.0 9.4 %all-to-all-done.1 = bf16[128,2,2304]{2,1,0:T(2,128)(2,1)S(1)} async-done(((bf16[128,2,2304]{2,1,0:T(2,128)(2,1)}), bf16[128,2,2304]{2,1,0:T(2,128)(2,1)S(1)}, u32[]{:S(2)}, u32[]{:S(2)}) %all-to-all-start.1) | async-done | bytes 1179680 | tf_op jit(solution)/shard_map/all_to_all | solution.py:403
  84.4 0.5 reshape.43.back
  84.9 4.3 %sample.1 = bf16[1024,256]{1,0:T(8,128)(2,1)S(1)} custom-call(bf16[256,2304]{1,0:T(8,128)(2,1)S(1)} %reshape.43.back, bf16[6,256,256]{2,1,0:T(8,128)(2,1)} %get-tuple-element.25.take_far, bf16[12,128,256]{2,1,0:T(8,128)(2,1)} %get-tuple-element.26.put_far, f32[2,256,256]{2,1,0:T(8,128)} %get-tuple-element.27.gate_rows_far, ...), custom_call_target="tpu_custom_call" | custom-call | flops 536870912 | bytes 1048576 | tf_op jit(solution)/shard_map/sample/pallas_call | solution.py:76
  89.2 24.6 %all_to_all.15 = bf16[128,8,256]{2,1,0:T(8,128)(2,1)S(1)} all-to-all(bf16[128,8,256]{2,1,0:T(8,128)(2,1)S(1)} %bitcast.9), channel_id=1, replica_groups=mesh['expert_0'=4,'expert_1'=8,'expert_2'=4,'dp'=2] {'expert_0','expert_..., dimensions={0} | all-to-all | bytes 1048576 | tf_op jit(solution)/shard_map/all_to_all | solution.py:403
  113.8 5.1 %collective-permute-start.1 = (bf16[1024,256]{1,0:T(8,128)(2,1)S(1)}, bf16[1024,256]{1,0:T(8,128)(2,1)S(1)}, u32[]{:S(2)}, u32[]{:S(2)}) collective-permute-start(bf16[1024,256]{1,0:T(8,128)(2,1)S(1)} %bitcast.10), channel_id=1, source_target_pairs={{0,1},{1,0},{2,3},{3,2},{4,5},{5,4},{6,7},{7,6},{8,9},{9,8},{10,11... | collective-permute-start | bytes 1572872 | tf_op jit(solution)/shard_map/ppermute | solution.py:408
  118.9 1.7 %own.1 = (bf16[768,512]{1,0:T(8,128)(2,1)S(1)}, bf16[768,256]{1,0:T(8,128)(2,1)S(1)}, f32[2,256]{1,0:T(2,128)S(1)}, f32[2,256]{1,0:T(2,128)S(1)}, f32[1024,256]{1,0:T(8,128)S(1)}) custom-call(bf16[256,768]{1,0:T(8,128)(2,1)S(1)} %copy-done.2, bf16[1024,256]{1,0:T(8,128)(2,1)S(1)} %bitcast.11, f32[2,256]{1,0:T(2,128)S(1)} %copy-done.3, f32[1024,256]{1,0:T(8,128)S(1)} %copy-done.6), custom_call_target="tpu_custom_call" | custom-call | flops 536870912 | bytes 1048576 | tf_op jit(solution)/shard_map/own/pallas_call | solution.py:76
  120.6 10.1 %final.1 = (f32[2048,256]{1,0:T(8,128)}, f32[2048,256]{1,0:T(8,128)}, f32[2,256]{1,0:T(2,128)}, f32[2,256]{1,0:T(2,128)}, f32[1024,256]{1,0:T(8,128)}) custom-call(bf16[256,768]{1,0:T(8,128)(2,1)S(1)} %copy-done.8, bf16[1024,256]{1,0:T(8,128)(2,1)S(1)} %collective-permute-done.1.got_other, bf16[768,512]{1,0:T(8,128)(2,1)S(1)} %get-tuple-element.33.scaled_own, ...), custom_call_target="tpu_custom_call" | custom-call | flops 6442450944 | bytes 1048576 | tf_op jit(solution)/shard_map/final/pallas_call | solution.py:76
  (27 shorter events, 0.1 us)
Async XLA Ops:
  2.8 31.2 %all-to-all-start = ((bf16[128,2,768]{2,1,0:T(2,128)(2,1)}), bf16[128,2,768]{2,1,0:T(2,128)(2,1)S(1)}, u32[]{:S(2)}, u32[]{:S(2)}) async-start(bf16[128,2,768]{2,1,0:T(2,128)(2,1)} %reshape.40), calls=%async_computation | async-start | bytes 786432 | tf_op jit(solution)/shard_map/all_to_all | solution.py:403
  34.1 21.3 %copy-start.1 = (bf16[256,768]{1,0:T(8,128)(2,1)}, bf16[256,768]{1,0:T(8,128)(2,1)S(1)}, u32[]{:S(2)}) copy-start(bf16[256,768]{1,0:T(8,128)(2,1)S(1)} %reshape.41.x) | copy-start | bytes 1179652
  34.1 1.7 %copy-start.5 = (bf16[1,4096,256]{2,1,0:T(8,128)(2,1)S(1)}, bf16[1,4096,256]{2,1,0:T(8,128)(2,1)}, u32[]{:S(2)}) copy-start(bf16[1,4096,256]{2,1,0:T(8,128)(2,1)} %param.15) | copy-start | bytes 6291460
  35.9 0.8 copy-start.9
  46.2 11.3 %copy-start.11 = (s32[256,2]{0,1:T(2,128)S(1)}, s32[256,2]{0,1:T(2,128)}, u32[]{:S(2)}) copy-start(s32[256,2]{0,1:T(2,128)} %param.13) | copy-start | bytes 6148
  46.3 12.1 %copy-start.13 = (s32[512]{0:T(512)S(1)}, s32[512]{0:T(512)}, u32[]{:S(2)}) copy-start(s32[512]{0:T(512)} %param.20) | copy-start | bytes 6148
  46.3 12.8 %copy-start.14 = (s32[512]{0:T(512)S(1)}, s32[512]{0:T(512)}, u32[]{:S(2)}) copy-start(s32[512]{0:T(512)} %param.21) | copy-start | bytes 6148
  46.3 13.5 %copy-start.15 = (f32[512]{0:T(512)S(1)}, f32[512]{0:T(512)}, u32[]{:S(2)}) copy-start(f32[512]{0:T(512)} %param.22) | copy-start | bytes 6148
  46.3 14.3 %copy-start.12 = (s32[256,2]{0,1:T(2,128)S(1)}, s32[256,2]{0,1:T(2,128)}, u32[]{:S(2)}) copy-start(s32[256,2]{0,1:T(2,128)} %param.14) | copy-start | bytes 6148
  46.3 15.0 %copy-start.10 = (bf16[128,2,256]{2,1,0:T(2,128)(2,1)S(1)}, bf16[128,2,256]{2,1,0:T(2,128)(2,1)}, u32[]{:S(2)}) copy-start(bf16[128,2,256]{2,1,0:T(2,128)(2,1)} %param.17) | copy-start | bytes 393220
  47.6 36.8 %all-to-all-start.1 = ((bf16[128,2,2304]{2,1,0:T(2,128)(2,1)}), bf16[128,2,2304]{2,1,0:T(2,128)(2,1)S(1)}, u32[]{:S(2)}, u32[]{:S(2)}) async-start(bf16[128,2,2304]{2,1,0:T(2,128)(2,1)} %reshape.42), calls=%async_computation.1 | async-start | bytes 2359296 | tf_op jit(solution)/shard_map/all_to_all | solution.py:403
  55.5 10.2 %collective-permute-start = (bf16[256,768]{1,0:T(8,128)(2,1)S(1)}, bf16[256,768]{1,0:T(8,128)(2,1)S(1)}, u32[]{:S(2)}, u32[]{:S(2)}) collective-permute-start(bf16[256,768]{1,0:T(8,128)(2,1)S(1)} %reshape.41.x), channel_id=1, source_target_pairs={{0,1},{1,0},{2,3},{3,2},{4,5},{5,4},{6,7},{7,6},{8,9},{9,8},{10,11... | collective-permute-start | bytes 1179656 | tf_op jit(solution)/shard_map/ppermute | solution.py:408
  65.7 0.8 copy-start.7
  75.0 9.9 %copy-start.3 = (f32[2,256]{1,0:T(2,128)S(1)}, f32[2,256]{1,0:T(2,128)}, u32[]{:S(2)}) copy-start(f32[2,256]{1,0:T(2,128)} %tower.9) | copy-start | bytes 6148
  75.0 9.9 %copy-start.4 = (f32[2]{0:T(128)S(1)}, f32[2]{0:T(128)}, u32[]{:S(2)}) copy-start(f32[2]{0:T(128)} %bias.1) | copy-start | bytes 28
  84.9 34.0 %copy-start.2 = (bf16[256,768]{1,0:T(8,128)(2,1)S(1)}, bf16[256,768]{1,0:T(8,128)(2,1)}, u32[]{:S(2)}) copy-start(bf16[256,768]{1,0:T(8,128)(2,1)} %copy-done.1) | copy-start | bytes 1179652
  84.9 34.0 %copy-start.6 = (f32[1024,256]{1,0:T(8,128)S(1)}, f32[1024,256]{1,0:T(8,128)}, u32[]{:S(2)}) copy-start(f32[1024,256]{1,0:T(8,128)} %table.1) | copy-start | bytes 3145732
  89.2 31.4 %copy-start = (f32[2048,128]{1,0:T(8,128)S(1)}, f32[2048,128]{1,0:T(8,128)}, u32[]{:S(2)}) copy-start(f32[2048,128]{1,0:T(8,128)} %get-tuple-element.32.after.slope) | copy-start | bytes 3145732
  89.2 31.4 %copy-start.8 = (bf16[256,768]{1,0:T(8,128)(2,1)S(1)}, bf16[256,768]{1,0:T(8,128)(2,1)}, u32[]{:S(2)}) copy-start(bf16[256,768]{1,0:T(8,128)(2,1)} %copy-done.7) | copy-start | bytes 1179652
  113.8 6.8 %collective-permute-start.1 = (bf16[1024,256]{1,0:T(8,128)(2,1)S(1)}, bf16[1024,256]{1,0:T(8,128)(2,1)S(1)}, u32[]{:S(2)}, u32[]{:S(2)}) collective-permute-start(bf16[1024,256]{1,0:T(8,128)(2,1)S(1)} %bitcast.10), channel_id=1, source_target_pairs={{0,1},{1,0},{2,3},{3,2},{4,5},{5,4},{6,7},{7,6},{8,9},{9,8},{10,11... | collective-permute-start | bytes 1572872 | tf_op jit(solution)/shard_map/ppermute | solution.py:408

commit v3 on v2

--- a/solution.py
+++ b/solution.py
@@ -15,7 +15,6 @@
 STEP_SIZE = 0.25
 BF = jnp.bfloat16
 F32 = jnp.float32
-CHUNK = 2048
 
 ROWS = 2
 BLOCKS = 3
@@ -171,34 +170,28 @@
         slopes[t : t + 1, :] = found[t : t + 1] + found[2 + t : 3 + t] + found[4 + t : 5 + t]
 
 
-def expert_kernel(x, w_in, w_out_far, slopes, out, total, stacked, w_out, sems):
+def expert_kernel(x, w_in, w_out, slopes, out, total, stacked):
+    step = pl.program_id(0)
     rows = x.shape[0]
-    hidden, feature = w_out.shape
+    feature = w_in.shape[1]
     wide = 3 * feature
-    units = [slice(at, at + CHUNK) for at in range(0, hidden, CHUNK)]
-    arrived = []
-    for n, unit in enumerate(units):
-        copy = pltpu.make_async_copy(w_out_far.at[unit, :], w_out.at[unit, :], sems.at[n])
-        copy.start()
-        arrived.append(copy)
-    for c in range(BLOCKS):
-        stacked[c * rows : (c + 1) * rows, :] = x[:, c * feature : (c + 1) * feature]
-    for n, unit in enumerate(units):
-        act, grad = silu_and_slope(dot_last(stacked[...], w_in[unit, :]))
-        parts = [
-            dot((grad * slopes[t : t + 1, unit]).astype(BF), w_in[unit, :]) for t in range(2)
-        ]
-        act = act.astype(BF)
-        arrived[n].wait()
-        parts = [dot(act, w_out[unit, :])] + parts
-        for p, part in enumerate(parts):
-            cols = slice(p * feature, (p + 1) * feature)
-            if n == 0:
-                total[:, cols] = part
-            else:
-                total[:, cols] += part
-    for c in range(BLOCKS):
-        out[:, c * wide : (c + 1) * wide] = total[c * rows : (c + 1) * rows, :].astype(BF)
+
+    @pl.when(step == 0)
+    def _():
+        total[...] = jnp.zeros_like(total)
+        for c in range(BLOCKS):
+            stacked[c * rows : (c + 1) * rows, :] = x[:, c * feature : (c + 1) * feature]
+
+    act, grad = silu_and_slope(dot_last(stacked[...], w_in[...]))
+    total[:, :feature] += dot(act.astype(BF), w_out[...])
+    for t in range(2):
+        cols = slice((1 + t) * feature, (2 + t) * feature)
+        total[:, cols] += dot((grad * slopes[t : t + 1, :]).astype(BF), w_in[...])
+
+    @pl.when(step == pl.num_programs(0) - 1)
+    def _():
+        for c in range(BLOCKS):
+            out[:, c * wide : (c + 1) * wide] = total[c * rows : (c + 1) * rows, :].astype(BF)
 
 
 def half_kernel(half, x, x_other, w_in, w_out, tower, act_t, grad_t, slope):
@@ -490,25 +483,30 @@
         (out_matrix, tower_weight),
         1 << 31,
         "slopes",
-        60,
+        12,
         grid=(hidden // depth,),
         in_specs=[pl.BlockSpec((depth, feature), lambda i: (i, 0)), full(tower_weight.shape)],
         out_specs=pl.BlockSpec((2, depth), lambda i: (0, i)),
     )
+    piece = hidden // 2
     message = call(
         expert_kernel,
         jax.ShapeDtypeStruct((rows, 3 * BLOCKS * feature), BF),
-        (received, in_matrix, far(out_matrix), slopes),
+        (received, far(in_matrix), far(out_matrix), slopes),
         7 << 30,
         "expert",
-        40,
-        in_specs=[in_vmem, in_vmem, in_hbm, in_vmem],
-        out_specs=in_vmem,
+        32,
+        grid=(hidden // piece,),
+        in_specs=[
+            full(received.shape),
+            pl.BlockSpec((piece, feature), lambda i: (i, 0)),
+            pl.BlockSpec((piece, feature), lambda i: (i, 0)),
+            pl.BlockSpec((2, piece), lambda i: (0, i)),
+        ],
+        out_specs=full((rows, 3 * BLOCKS * feature)),
         scratch_shapes=[
             pltpu.VMEM((BLOCKS * rows, 3 * feature), F32),
             pltpu.VMEM((BLOCKS * rows, feature), BF),
-            pltpu.VMEM((hidden, feature), BF),
-            pltpu.SemaphoreType.DMA((hidden // CHUNK,)),
         ],
     )
     returned = exchanged(message, ROWS)

time: 131 us -> 129 us (0.985)
  Pallas kernels: 41.7 us -> 40 us
    pallas_call x8, Pallas kernels: 41.7 us -> 40 us  [call(): pl.pallas_call(kernel, out_shape=out_shape, cost_estimate=pl.CostEstimate...]
  transfers between devices with their start and end apart: 4 -> 4, of which waited for: 2 -> 2; matrix products, arithmetic and copies ran while one was open for 3% -> 3% of each run, Pallas kernels for 13% -> 11%
where the time goes in v3:
time: 129 us; the launch traced here: 128 us
  Pallas kernels  40 us (31%)
  starting transfers between devices  31.4 us (24%)
  blocking collectives  24.6 us (19%)
  waiting for transfers between devices  21.6 us (17%)
  local copies, waits for them, and re-layouts  9.69 us (8%)
    pallas_call x8, Pallas kernels, call(): pl.pallas_call(kernel, out_shape=out_shape, cost_estimate=pl.CostEstimate...  40 us
    all_to_all x1, blocking collectives, exchanged(): lax.all_to_all(rows.reshape(-1, each, width), EXPERT, split_axis=0, conca...  24.6 us
    all_to_all x2, starting transfers between devices, exchanged(): lax.all_to_all(rows.reshape(-1, each, width), EXPERT, split_axis=0, conca...  24 us
    all_to_all x2, waiting for transfers between devices, exchanged(): lax.all_to_all(rows.reshape(-1, each, width), EXPERT, split_axis=0, conca...  21.6 us
    ppermute x2, starting transfers between devices, swapped(): return lax.ppermute(shard, 'dp', [(0, 1), (1, 0)])  7.35 us
    unnamed x34, local copies, waits for them, and re-layouts  4.01 us
  transfers between devices with their start and end apart: 4, of which 2 were waited for; matrix products, arithmetic and copies ran while one was open for 3% of the time, Pallas kernels for 11%

profile of v3, /device:TPU:1, one launch (start us, length us, event | category | flops | bytes accessed | tf_op | source)
XLA Modules:
  0.0 128.3 jit_solution(5168491985225978326)
XLA Ops:
  0.6 0.0 copy-start.3
  0.6 1.3 dispatch.1
  1.9 0.9 reshape.40
  2.8 16.3 %all-to-all-start = ((bf16[128,2,768]{2,1,0:T(2,128)(2,1)}), bf16[128,2,768]{2,1,0:T(2,128)(2,1)S(1)}, u32[]{:S(2)}, u32[]{:S(2)}) async-start(bf16[128,2,768]{2,1,0:T(2,128)(2,1)} %reshape.40), calls=%async_computation | async-start | bytes 786432 | tf_op jit(solution)/shard_map/all_to_all | solution.py:396
  19.2 0.0 copy-start.6
  19.2 1.6 %copy-done.6 = bf16[1,4096,256]{2,1,0:T(8,128)(2,1)S(1)} copy-done((bf16[1,4096,256]{2,1,0:T(8,128)(2,1)S(1)}, bf16[1,4096,256]{2,1,0:T(8,128)(2,1)}, u32[]{:S(2)}) %copy-start.6) | copy-done | bytes 2097176
  20.8 0.8 slopes.1
  21.6 12.4 %all-to-all-done = bf16[128,2,768]{2,1,0:T(2,128)(2,1)S(1)} async-done(((bf16[128,2,768]{2,1,0:T(2,128)(2,1)}), bf16[128,2,768]{2,1,0:T(2,128)(2,1)S(1)}, u32[]{:S(2)}, u32[]{:S(2)}) %all-to-all-start) | async-done | bytes 393248 | tf_op jit(solution)/shard_map/all_to_all | solution.py:396
  34.0 0.1 reshape.41.x
  34.2 9.7 %expert.1 = bf16[256,2304]{1,0:T(8,128)(2,1)S(1)} custom-call(bf16[256,768]{1,0:T(8,128)(2,1)S(1)} %reshape.41.x, bf16[4096,256]{1,0:T(8,128)(2,1)} %bitcast.17, bf16[4096,256]{1,0:T(8,128)(2,1)} %bitcast.12, f32[2,4096]{1,0:T(2,128)S(1)} %slopes.1), custom_call_target="tpu_custom_call" | custom-call | flops 7516192768 | bytes 1048576 | tf_op jit(solution)/shard_map/expert/pallas_call | solution.py:75
  43.9 0.0 copy-start.11
  43.9 0.0 copy-start.14
  43.9 0.0 copy-start.15
  44.0 1.3 %reshape.42 = bf16[128,2,2304]{2,1,0:T(2,128)(2,1)} reshape(bf16[256,2304]{1,0:T(8,128)(2,1)S(1)} %expert.1) | data formatting | bytes 2359296 | tf_op jit(solution)/shard_map/reshape | solution.py:396
  45.3 7.7 %all-to-all-start.1 = ((bf16[128,2,2304]{2,1,0:T(2,128)(2,1)}), bf16[128,2,2304]{2,1,0:T(2,128)(2,1)S(1)}, u32[]{:S(2)}, u32[]{:S(2)}) async-start(bf16[128,2,2304]{2,1,0:T(2,128)(2,1)} %reshape.42), calls=%async_computation.1 | async-start | bytes 2359296 | tf_op jit(solution)/shard_map/all_to_all | solution.py:396
  52.9 2.3 %collective-permute-start = (bf16[256,768]{1,0:T(8,128)(2,1)S(1)}, bf16[256,768]{1,0:T(8,128)(2,1)S(1)}, u32[]{:S(2)}, u32[]{:S(2)}) collective-permute-start(bf16[256,768]{1,0:T(8,128)(2,1)S(1)} %reshape.41.x), channel_id=1, source_target_pairs={{0,1},{1,0},{2,3},{3,2},{4,5},{5,4},{6,7},{7,6},{8,9},{9,8},{10,11... | collective-permute-start | bytes 1179656 | tf_op jit(solution)/shard_map/ppermute | solution.py:401
  55.2 0.8 copy.19.routes
  56.0 0.7 reshape.45.bag_rows
  56.8 0.7 reshape.46.bag_sample
  57.5 0.7 reshape.47.bag_weight
  58.2 0.8 copy.20.labels
  59.0 0.7 reshape.44.gate_flat
  59.7 3.6 %prepare.1 = (bf16[6,256,256]{2,1,0:T(8,128)(2,1)}, bf16[12,128,256]{2,1,0:T(8,128)(2,1)}, f32[2,256,256]{2,1,0:T(8,128)}, f32[2,256,128]{2,1,0:T(8,128)}, f32[1...) custom-call(s32[256,2]{1,0:T(8,128)} %copy.19.routes, s32[2,256]{1,0:T(2,128)} %bitcast.16, ...), custom_call_target="tpu_custom_call" | custom-call | flops 2147483648 | bytes 1048576 | tf_op jit(solution)/shard_map/prepare/pallas_call | solution.py:75
  63.3 0.8 copy-done.8
  64.1 8.6 %half.1 = (bf16[2048,1536]{1,0:T(8,128)(2,1)}, bf16[2048,1536]{1,0:T(8,128)(2,1)}, f32[2048,128]{1,0:T(8,128)}) custom-call(s32[1]{0:T(128)} %bitcast.3.half, bf16[256,768]{1,0:T(8,128)(2,1)} %copy-done.1, bf16[256,768]{1,0:T(8,128)(2,1)} %copy-done.8, bf16[4096,256]{1,0:T(8,128)(2,1)} %bitcast.18, bf16[4096,256]{1,0:T(8,128)(2,1)} %bitcast.13, f32[2,256]{1,0:T(2,128)} %tower.9), custom_call_target="tpu_custom_call" | custom-call | flops 7516192768 | bytes 1048576 | tf_op jit(solution)/shard_map/half/pallas_call | solution.py:75
  72.7 9.2 %all-to-all-done.1 = bf16[128,2,2304]{2,1,0:T(2,128)(2,1)S(1)} async-done(((bf16[128,2,2304]{2,1,0:T(2,128)(2,1)}), bf16[128,2,2304]{2,1,0:T(2,128)(2,1)S(1)}, u32[]{:S(2)}, u32[]{:S(2)}) %all-to-all-start.1) | async-done | bytes 1179680 | tf_op jit(solution)/shard_map/all_to_all | solution.py:396
  81.9 0.5 reshape.43.back
  82.4 4.3 %sample.1 = bf16[1024,256]{1,0:T(8,128)(2,1)S(1)} custom-call(bf16[256,2304]{1,0:T(8,128)(2,1)S(1)} %reshape.43.back, bf16[6,256,256]{2,1,0:T(8,128)(2,1)} %get-tuple-element.25.take_far, bf16[12,128,256]{2,1,0:T(8,128)(2,1)} %get-tuple-element.26.put_far, f32[2,256,256]{2,1,0:T(8,128)} %get-tuple-element.27.gate_rows_far, ...), custom_call_target="tpu_custom_call" | custom-call | flops 536870912 | bytes 1048576 | tf_op jit(solution)/shard_map/sample/pallas_call | solution.py:75
  86.7 24.6 %all_to_all.15 = bf16[128,8,256]{2,1,0:T(8,128)(2,1)S(1)} all-to-all(bf16[128,8,256]{2,1,0:T(8,128)(2,1)S(1)} %bitcast.9), channel_id=1, replica_groups=mesh['expert_0'=4,'expert_1'=8,'expert_2'=4,'dp'=2] {'expert_0','expert_..., dimensions={0} | all-to-all | bytes 1048576 | tf_op jit(solution)/shard_map/all_to_all | solution.py:396
  111.3 5.1 %collective-permute-start.1 = (bf16[1024,256]{1,0:T(8,128)(2,1)S(1)}, bf16[1024,256]{1,0:T(8,128)(2,1)S(1)}, u32[]{:S(2)}, u32[]{:S(2)}) collective-permute-start(bf16[1024,256]{1,0:T(8,128)(2,1)S(1)} %bitcast.10), channel_id=1, source_target_pairs={{0,1},{1,0},{2,3},{3,2},{4,5},{5,4},{6,7},{7,6},{8,9},{9,8},{10,11... | collective-permute-start | bytes 1572872 | tf_op jit(solution)/shard_map/ppermute | solution.py:401
  116.4 1.7 %own.1 = (bf16[768,512]{1,0:T(8,128)(2,1)S(1)}, bf16[768,256]{1,0:T(8,128)(2,1)S(1)}, f32[2,256]{1,0:T(2,128)S(1)}, f32[2,256]{1,0:T(2,128)S(1)}, f32[1024,256]{1,0:T(8,128)S(1)}) custom-call(bf16[256,768]{1,0:T(8,128)(2,1)S(1)} %copy-done.2, bf16[1024,256]{1,0:T(8,128)(2,1)S(1)} %bitcast.11, f32[2,256]{1,0:T(2,128)S(1)} %copy-done.4, f32[1024,256]{1,0:T(8,128)S(1)} %copy-done.7), custom_call_target="tpu_custom_call" | custom-call | flops 536870912 | bytes 1048576 | tf_op jit(solution)/shard_map/own/pallas_call | solution.py:75
  118.1 10.1 %final.1 = (f32[2048,256]{1,0:T(8,128)}, f32[2048,256]{1,0:T(8,128)}, f32[2,256]{1,0:T(2,128)}, f32[2,256]{1,0:T(2,128)}, f32[1024,256]{1,0:T(8,128)}) custom-call(bf16[256,768]{1,0:T(8,128)(2,1)S(1)} %copy-done.9, bf16[1024,256]{1,0:T(8,128)(2,1)S(1)} %collective-permute-done.1.got_other, bf16[768,512]{1,0:T(8,128)(2,1)S(1)} %get-tuple-element.33.scaled_own, ...), custom_call_target="tpu_custom_call" | custom-call | flops 6442450944 | bytes 1048576 | tf_op jit(solution)/shard_map/final/pallas_call | solution.py:75
  (27 shorter events, 0.1 us)
Async XLA Ops:
  0.6 18.5 %copy-start.3 = (f32[2,256]{1,0:T(2,128)S(1)}, f32[2,256]{1,0:T(2,128)}, u32[]{:S(2)}) copy-start(f32[2,256]{1,0:T(2,128)} %tower.9) | copy-start | bytes 6148
  2.8 31.2 %all-to-all-start = ((bf16[128,2,768]{2,1,0:T(2,128)(2,1)}), bf16[128,2,768]{2,1,0:T(2,128)(2,1)S(1)}, u32[]{:S(2)}, u32[]{:S(2)}) async-start(bf16[128,2,768]{2,1,0:T(2,128)(2,1)} %reshape.40), calls=%async_computation | async-start | bytes 786432 | tf_op jit(solution)/shard_map/all_to_all | solution.py:396
  19.2 1.6 %copy-start.6 = (bf16[1,4096,256]{2,1,0:T(8,128)(2,1)S(1)}, bf16[1,4096,256]{2,1,0:T(8,128)(2,1)}, u32[]{:S(2)}) copy-start(bf16[1,4096,256]{2,1,0:T(8,128)(2,1)} %param.16) | copy-start | bytes 6291460
  34.1 18.8 %copy-start.1 = (bf16[256,768]{1,0:T(8,128)(2,1)}, bf16[256,768]{1,0:T(8,128)(2,1)S(1)}, u32[]{:S(2)}) copy-start(bf16[256,768]{1,0:T(8,128)(2,1)S(1)} %reshape.41.x) | copy-start | bytes 1179652
  43.9 11.3 %copy-start.11 = (s32[256,2]{0,1:T(2,128)S(1)}, s32[256,2]{0,1:T(2,128)}, u32[]{:S(2)}) copy-start(s32[256,2]{0,1:T(2,128)} %param.13) | copy-start | bytes 6148
  43.9 12.1 %copy-start.13 = (s32[512]{0:T(512)S(1)}, s32[512]{0:T(512)}, u32[]{:S(2)}) copy-start(s32[512]{0:T(512)} %param.20) | copy-start | bytes 6148
  43.9 12.8 %copy-start.14 = (s32[512]{0:T(512)S(1)}, s32[512]{0:T(512)}, u32[]{:S(2)}) copy-start(s32[512]{0:T(512)} %param.21) | copy-start | bytes 6148
  43.9 13.6 %copy-start.15 = (f32[512]{0:T(512)S(1)}, f32[512]{0:T(512)}, u32[]{:S(2)}) copy-start(f32[512]{0:T(512)} %param.22) | copy-start | bytes 6148
  43.9 14.3 %copy-start.12 = (s32[256,2]{0,1:T(2,128)S(1)}, s32[256,2]{0,1:T(2,128)}, u32[]{:S(2)}) copy-start(s32[256,2]{0,1:T(2,128)} %param.14) | copy-start | bytes 6148
  44.0 15.1 %copy-start.10 = (bf16[128,2,256]{2,1,0:T(2,128)(2,1)S(1)}, bf16[128,2,256]{2,1,0:T(2,128)(2,1)}, u32[]{:S(2)}) copy-start(bf16[128,2,256]{2,1,0:T(2,128)(2,1)} %param.17) | copy-start | bytes 393220
  45.3 36.6 %all-to-all-start.1 = ((bf16[128,2,2304]{2,1,0:T(2,128)(2,1)}), bf16[128,2,2304]{2,1,0:T(2,128)(2,1)S(1)}, u32[]{:S(2)}, u32[]{:S(2)}) async-start(bf16[128,2,2304]{2,1,0:T(2,128)(2,1)} %reshape.42), calls=%async_computation.1 | async-start | bytes 2359296 | tf_op jit(solution)/shard_map/all_to_all | solution.py:396
  52.9 10.4 %collective-permute-start = (bf16[256,768]{1,0:T(8,128)(2,1)S(1)}, bf16[256,768]{1,0:T(8,128)(2,1)S(1)}, u32[]{:S(2)}, u32[]{:S(2)}) collective-permute-start(bf16[256,768]{1,0:T(8,128)(2,1)S(1)} %reshape.41.x), channel_id=1, source_target_pairs={{0,1},{1,0},{2,3},{3,2},{4,5},{5,4},{6,7},{7,6},{8,9},{9,8},{10,11... | collective-permute-start | bytes 1179656 | tf_op jit(solution)/shard_map/ppermute | solution.py:401
  63.3 0.8 copy-start.8
  72.7 9.7 %copy-start.4 = (f32[2,256]{1,0:T(2,128)S(1)}, f32[2,256]{1,0:T(2,128)}, u32[]{:S(2)}) copy-start(f32[2,256]{1,0:T(2,128)} %tower.9) | copy-start | bytes 6148
  72.7 9.7 %copy-start.5 = (f32[2]{0:T(128)S(1)}, f32[2]{0:T(128)}, u32[]{:S(2)}) copy-start(f32[2]{0:T(128)} %bias.1) | copy-start | bytes 28
  82.4 34.0 %copy-start.2 = (bf16[256,768]{1,0:T(8,128)(2,1)S(1)}, bf16[256,768]{1,0:T(8,128)(2,1)}, u32[]{:S(2)}) copy-start(bf16[256,768]{1,0:T(8,128)(2,1)} %copy-done.1) | copy-start | bytes 1179652
  82.4 34.0 %copy-start.7 = (f32[1024,256]{1,0:T(8,128)S(1)}, f32[1024,256]{1,0:T(8,128)}, u32[]{:S(2)}) copy-start(f32[1024,256]{1,0:T(8,128)} %table.1) | copy-start | bytes 3145732
  86.7 31.4 %copy-start = (f32[2048,128]{1,0:T(8,128)S(1)}, f32[2048,128]{1,0:T(8,128)}, u32[]{:S(2)}) copy-start(f32[2048,128]{1,0:T(8,128)} %get-tuple-element.32.after.slope) | copy-start | bytes 3145732
  86.7 31.4 %copy-start.9 = (bf16[256,768]{1,0:T(8,128)(2,1)S(1)}, bf16[256,768]{1,0:T(8,128)(2,1)}, u32[]{:S(2)}) copy-start(bf16[256,768]{1,0:T(8,128)(2,1)} %copy-done.8) | copy-start | bytes 1179652
  111.3 6.8 %collective-permute-start.1 = (bf16[1024,256]{1,0:T(8,128)(2,1)S(1)}, bf16[1024,256]{1,0:T(8,128)(2,1)S(1)}, u32[]{:S(2)}, u32[]{:S(2)}) collective-permute-start(bf16[1024,256]{1,0:T(8,128)(2,1)S(1)} %bitcast.10), channel_id=1, source_target_pairs={{0,1},{1,0},{2,3},{3,2},{4,5},{5,4},{6,7},{7,6},{8,9},{9,8},{10,11... | collective-permute-start | bytes 1572872 | tf_op jit(solution)/shard_map/ppermute | solution.py:401

commit v4 on v3

--- a/solution.py
+++ b/solution.py
@@ -117,7 +117,7 @@
     first = (BLOCKS * (row & 1)).astype(F32)
     for k in range(2):
         for c in range(BLOCKS):
-            take[BLOCKS * k + c] = ones_where(named[k] & (rank == first + c))
+            take[k, :, c * rows : (c + 1) * rows] = ones_where(named[k] & (rank == first + c))
     owner = iota((owners, tok), 0)
     named_t = [owner == routes_t[k : k + 1, :] for k in range(2)]
     later = ones_where(iota((tok, tok), 0) < iota((tok, tok), 1))
@@ -217,7 +217,7 @@
 def sample_kernel(
     back, take_far, put_far, gate_rows_far, lanes_far, side_far, bag_pick_far, bag_scale_far,
     tower, bias, after,
-    out, take, put, gate_rows, lanes, side, bag_pick, bag_scale, sems,
+    out, take, put, gate_rows, lanes, side, bag_pick, bag_scale, stacked, sems,
 ):
     del after
     pairs = (
@@ -234,13 +234,11 @@
         copy.start()
     feature = tower.shape[1]
     wide = 3 * feature
-    parts = []
+    rows = back.shape[0]
+    for c in range(BLOCKS):
+        stacked[c * rows : (c + 1) * rows, :] = back[:, c * wide : (c + 1) * wide]
     copies[0].wait()
-    for k in range(2):
-        part = dot(take[BLOCKS * k], back[:, :wide])
-        for c in range(1, BLOCKS):
-            part += dot(take[BLOCKS * k + c], back[:, c * wide : (c + 1) * wide])
-        parts.append(part)
+    parts = [dot(take[k], stacked[...]) for k in range(2)]
     task_row = iota((128, feature), 0)
     weights = [
         jnp.where(task_row == 0, piece[0:1].astype(F32), jnp.where(task_row == 1, piece[1:2].astype(F32), 0.0)).astype(BF)
@@ -454,7 +452,7 @@
     take, put, gate_rows, lanes, side, bag_pick, bag_scale = call(
         prepare_kernel,
         shapes(
-            ((2 * BLOCKS, tok, rows), BF),
+            ((2, tok, BLOCKS * rows), BF),
             ((2 * SLOTS, owners, tok), BF),
             ((2, tok, feature), F32),
             ((2, tok, 128), F32),
@@ -568,6 +566,7 @@
             pltpu.VMEM(side.shape, F32),
             pltpu.VMEM(bag_pick.shape, BF),
             pltpu.VMEM(bag_scale.shape, F32),
+            pltpu.VMEM((BLOCKS * rows, 3 * feature), BF),
             pltpu.SemaphoreType.DMA((7,)),
         ],
     )

time: 129 us -> 129 us (level)
  transfers between devices with their start and end apart: 4 -> 4, of which waited for: 2 -> 2; matrix products, arithmetic and copies ran while one was open for 3% -> 3% of each run, Pallas kernels for 11% -> 12%
where the time goes in v4:
time: 129 us; the launch traced here: 128 us
  Pallas kernels  40 us (31%)
  starting transfers between devices  31.4 us (24%)
  blocking collectives  24.6 us (19%)
  waiting for transfers between devices  21.5 us (17%)
  local copies, waits for them, and re-layouts  9.69 us (8%)
    pallas_call x8, Pallas kernels, call(): pl.pallas_call(kernel, out_shape=out_shape, cost_estimate=pl.CostEstimate...  40 us
    all_to_all x1, blocking collectives, exchanged(): lax.all_to_all(rows.reshape(-1, each, width), EXPERT, split_axis=0, conca...  24.6 us
    all_to_all x2, starting transfers between devices, exchanged(): lax.all_to_all(rows.reshape(-1, each, width), EXPERT, split_axis=0, conca...  24 us
    all_to_all x2, waiting for transfers between devices, exchanged(): lax.all_to_all(rows.reshape(-1, each, width), EXPERT, split_axis=0, conca...  21.5 us
    ppermute x2, starting transfers between devices, swapped(): return lax.ppermute(shard, 'dp', [(0, 1), (1, 0)])  7.36 us
    unnamed x34, local copies, waits for them, and re-layouts  4.01 us
  transfers between devices with their start and end apart: 4, of which 2 were waited for; matrix products, arithmetic and copies ran while one was open for 3% of the time, Pallas kernels for 12%

profile of v4, /device:TPU:1, one launch (start us, length us, event | category | flops | bytes accessed | tf_op | source)
XLA Modules:
  0.0 128.2 jit_solution(1867137008634176447)
XLA Ops:
  0.6 0.0 copy-start.3
  0.6 1.3 dispatch.1
  1.9 0.9 reshape.40
  2.8 16.3 %all-to-all-start = ((bf16[128,2,768]{2,1,0:T(2,128)(2,1)}), bf16[128,2,768]{2,1,0:T(2,128)(2,1)S(1)}, u32[]{:S(2)}, u32[]{:S(2)}) async-start(bf16[128,2,768]{2,1,0:T(2,128)(2,1)} %reshape.40), calls=%async_computation | async-start | bytes 786432 | tf_op jit(solution)/shard_map/all_to_all | solution.py:394
  19.2 0.0 copy-start.6
  19.2 1.6 %copy-done.6 = bf16[1,4096,256]{2,1,0:T(8,128)(2,1)S(1)} copy-done((bf16[1,4096,256]{2,1,0:T(8,128)(2,1)S(1)}, bf16[1,4096,256]{2,1,0:T(8,128)(2,1)}, u32[]{:S(2)}) %copy-start.6) | copy-done | bytes 2097176
  20.8 0.8 slopes.1
  21.6 12.4 %all-to-all-done = bf16[128,2,768]{2,1,0:T(2,128)(2,1)S(1)} async-done(((bf16[128,2,768]{2,1,0:T(2,128)(2,1)}), bf16[128,2,768]{2,1,0:T(2,128)(2,1)S(1)}, u32[]{:S(2)}, u32[]{:S(2)}) %all-to-all-start) | async-done | bytes 393248 | tf_op jit(solution)/shard_map/all_to_all | solution.py:394
  34.0 0.1 reshape.41.x
  34.2 9.7 %expert.1 = bf16[256,2304]{1,0:T(8,128)(2,1)S(1)} custom-call(bf16[256,768]{1,0:T(8,128)(2,1)S(1)} %reshape.41.x, bf16[4096,256]{1,0:T(8,128)(2,1)} %bitcast.17, bf16[4096,256]{1,0:T(8,128)(2,1)} %bitcast.12, f32[2,4096]{1,0:T(2,128)S(1)} %slopes.1), custom_call_target="tpu_custom_call" | custom-call | flops 7516192768 | bytes 1048576 | tf_op jit(solution)/shard_map/expert/pallas_call | solution.py:75
  43.9 0.0 copy-start.13
  43.9 0.0 copy-start.14
  44.0 0.0 copy-start.10
  44.0 1.3 %reshape.42 = bf16[128,2,2304]{2,1,0:T(2,128)(2,1)} reshape(bf16[256,2304]{1,0:T(8,128)(2,1)S(1)} %expert.1) | data formatting | bytes 2359296 | tf_op jit(solution)/shard_map/reshape | solution.py:394
  45.3 7.7 %all-to-all-start.1 = ((bf16[128,2,2304]{2,1,0:T(2,128)(2,1)}), bf16[128,2,2304]{2,1,0:T(2,128)(2,1)S(1)}, u32[]{:S(2)}, u32[]{:S(2)}) async-start(bf16[128,2,2304]{2,1,0:T(2,128)(2,1)} %reshape.42), calls=%async_computation.1 | async-start | bytes 2359296 | tf_op jit(solution)/shard_map/all_to_all | solution.py:394
  52.9 2.3 %collective-permute-start = (bf16[256,768]{1,0:T(8,128)(2,1)S(1)}, bf16[256,768]{1,0:T(8,128)(2,1)S(1)}, u32[]{:S(2)}, u32[]{:S(2)}) collective-permute-start(bf16[256,768]{1,0:T(8,128)(2,1)S(1)} %reshape.41.x), channel_id=1, source_target_pairs={{0,1},{1,0},{2,3},{3,2},{4,5},{5,4},{6,7},{7,6},{8,9},{9,8},{10,11... | collective-permute-start | bytes 1179656 | tf_op jit(solution)/shard_map/ppermute | solution.py:399
  55.2 0.8 copy.19.routes
  56.0 0.7 reshape.45.bag_rows
  56.8 0.7 reshape.46.bag_sample
  57.5 0.7 reshape.47.bag_weight
  58.2 0.8 copy.20.labels
  59.0 0.7 reshape.44.gate_flat
  59.7 3.7 %prepare.1 = (bf16[2,256,768]{2,1,0:T(8,128)(2,1)}, bf16[12,128,256]{2,1,0:T(8,128)(2,1)}, f32[2,256,256]{2,1,0:T(8,128)}, f32[2,256,128]{2,1,0:T(8,128)}, f32[1...) custom-call(s32[256,2]{1,0:T(8,128)} %copy.19.routes, s32[2,256]{1,0:T(2,128)} %bitcast.16, ...), custom_call_target="tpu_custom_call" | custom-call | flops 2147483648 | bytes 1048576 | tf_op jit(solution)/shard_map/prepare/pallas_call | solution.py:75
  63.4 0.8 copy-done.8
  64.2 8.6 %half.1 = (bf16[2048,1536]{1,0:T(8,128)(2,1)}, bf16[2048,1536]{1,0:T(8,128)(2,1)}, f32[2048,128]{1,0:T(8,128)}) custom-call(s32[1]{0:T(128)} %bitcast.3.half, bf16[256,768]{1,0:T(8,128)(2,1)} %copy-done.1, bf16[256,768]{1,0:T(8,128)(2,1)} %copy-done.8, bf16[4096,256]{1,0:T(8,128)(2,1)} %bitcast.18, bf16[4096,256]{1,0:T(8,128)(2,1)} %bitcast.13, f32[2,256]{1,0:T(2,128)} %tower.9), custom_call_target="tpu_custom_call" | custom-call | flops 7516192768 | bytes 1048576 | tf_op jit(solution)/shard_map/half/pallas_call | solution.py:75
  72.8 9.1 %all-to-all-done.1 = bf16[128,2,2304]{2,1,0:T(2,128)(2,1)S(1)} async-done(((bf16[128,2,2304]{2,1,0:T(2,128)(2,1)}), bf16[128,2,2304]{2,1,0:T(2,128)(2,1)S(1)}, u32[]{:S(2)}, u32[]{:S(2)}) %all-to-all-start.1) | async-done | bytes 1179680 | tf_op jit(solution)/shard_map/all_to_all | solution.py:394
  81.9 0.5 reshape.43.back
  82.4 4.2 %sample.1 = bf16[1024,256]{1,0:T(8,128)(2,1)S(1)} custom-call(bf16[256,2304]{1,0:T(8,128)(2,1)S(1)} %reshape.43.back, bf16[2,256,768]{2,1,0:T(8,128)(2,1)} %get-tuple-element.25.take_far, bf16[12,128,256]{2,1,0:T(8,128)(2,1)} %get-tuple-element.26.put_far, f32[2,256,256]{2,1,0:T(8,128)} %get-tuple-element.27.gate_rows_far, ...), custom_call_target="tpu_custom_call" | custom-call | flops 536870912 | bytes 1048576 | tf_op jit(solution)/shard_map/sample/pallas_call | solution.py:75
  86.6 24.6 %all_to_all.15 = bf16[128,8,256]{2,1,0:T(8,128)(2,1)S(1)} all-to-all(bf16[128,8,256]{2,1,0:T(8,128)(2,1)S(1)} %bitcast.9), channel_id=1, replica_groups=mesh['expert_0'=4,'expert_1'=8,'expert_2'=4,'dp'=2] {'expert_0','expert_..., dimensions={0} | all-to-all | bytes 1048576 | tf_op jit(solution)/shard_map/all_to_all | solution.py:394
  111.2 5.1 %collective-permute-start.1 = (bf16[1024,256]{1,0:T(8,128)(2,1)S(1)}, bf16[1024,256]{1,0:T(8,128)(2,1)S(1)}, u32[]{:S(2)}, u32[]{:S(2)}) collective-permute-start(bf16[1024,256]{1,0:T(8,128)(2,1)S(1)} %bitcast.10), channel_id=1, source_target_pairs={{0,1},{1,0},{2,3},{3,2},{4,5},{5,4},{6,7},{7,6},{8,9},{9,8},{10,11... | collective-permute-start | bytes 1572872 | tf_op jit(solution)/shard_map/ppermute | solution.py:399
  116.2 1.7 %own.1 = (bf16[768,512]{1,0:T(8,128)(2,1)S(1)}, bf16[768,256]{1,0:T(8,128)(2,1)S(1)}, f32[2,256]{1,0:T(2,128)S(1)}, f32[2,256]{1,0:T(2,128)S(1)}, f32[1024,256]{1,0:T(8,128)S(1)}) custom-call(bf16[256,768]{1,0:T(8,128)(2,1)S(1)} %copy-done.2, bf16[1024,256]{1,0:T(8,128)(2,1)S(1)} %bitcast.11, f32[2,256]{1,0:T(2,128)S(1)} %copy-done.4, f32[1024,256]{1,0:T(8,128)S(1)} %copy-done.7), custom_call_target="tpu_custom_call" | custom-call | flops 536870912 | bytes 1048576 | tf_op jit(solution)/shard_map/own/pallas_call | solution.py:75
  118.0 10.1 %final.1 = (f32[2048,256]{1,0:T(8,128)}, f32[2048,256]{1,0:T(8,128)}, f32[2,256]{1,0:T(2,128)}, f32[2,256]{1,0:T(2,128)}, f32[1024,256]{1,0:T(8,128)}) custom-call(bf16[256,768]{1,0:T(8,128)(2,1)S(1)} %copy-done.9, bf16[1024,256]{1,0:T(8,128)(2,1)S(1)} %collective-permute-done.1.got_other, bf16[768,512]{1,0:T(8,128)(2,1)S(1)} %get-tuple-element.33.scaled_own, ...), custom_call_target="tpu_custom_call" | custom-call | flops 6442450944 | bytes 1048576 | tf_op jit(solution)/shard_map/final/pallas_call | solution.py:75
  (27 shorter events, 0.1 us)
Async XLA Ops:
  0.6 18.5 %copy-start.3 = (f32[2,256]{1,0:T(2,128)S(1)}, f32[2,256]{1,0:T(2,128)}, u32[]{:S(2)}) copy-start(f32[2,256]{1,0:T(2,128)} %tower.9) | copy-start | bytes 6148
  2.8 31.2 %all-to-all-start = ((bf16[128,2,768]{2,1,0:T(2,128)(2,1)}), bf16[128,2,768]{2,1,0:T(2,128)(2,1)S(1)}, u32[]{:S(2)}, u32[]{:S(2)}) async-start(bf16[128,2,768]{2,1,0:T(2,128)(2,1)} %reshape.40), calls=%async_computation | async-start | bytes 786432 | tf_op jit(solution)/shard_map/all_to_all | solution.py:394
  19.2 1.6 %copy-start.6 = (bf16[1,4096,256]{2,1,0:T(8,128)(2,1)S(1)}, bf16[1,4096,256]{2,1,0:T(8,128)(2,1)}, u32[]{:S(2)}) copy-start(bf16[1,4096,256]{2,1,0:T(8,128)(2,1)} %param.16) | copy-start | bytes 6291460
  34.1 18.8 %copy-start.1 = (bf16[256,768]{1,0:T(8,128)(2,1)}, bf16[256,768]{1,0:T(8,128)(2,1)S(1)}, u32[]{:S(2)}) copy-start(bf16[256,768]{1,0:T(8,128)(2,1)S(1)} %reshape.41.x) | copy-start | bytes 1179652
  43.9 11.3 %copy-start.11 = (s32[256,2]{0,1:T(2,128)S(1)}, s32[256,2]{0,1:T(2,128)}, u32[]{:S(2)}) copy-start(s32[256,2]{0,1:T(2,128)} %param.13) | copy-start | bytes 6148
  43.9 12.1 %copy-start.13 = (s32[512]{0:T(512)S(1)}, s32[512]{0:T(512)}, u32[]{:S(2)}) copy-start(s32[512]{0:T(512)} %param.20) | copy-start | bytes 6148
  43.9 12.8 %copy-start.14 = (s32[512]{0:T(512)S(1)}, s32[512]{0:T(512)}, u32[]{:S(2)}) copy-start(s32[512]{0:T(512)} %param.21) | copy-start | bytes 6148
  43.9 13.6 %copy-start.15 = (f32[512]{0:T(512)S(1)}, f32[512]{0:T(512)}, u32[]{:S(2)}) copy-start(f32[512]{0:T(512)} %param.22) | copy-start | bytes 6148
  43.9 14.3 %copy-start.12 = (s32[256,2]{0,1:T(2,128)S(1)}, s32[256,2]{0,1:T(2,128)}, u32[]{:S(2)}) copy-start(s32[256,2]{0,1:T(2,128)} %param.14) | copy-start | bytes 6148
  44.0 15.1 %copy-start.10 = (bf16[128,2,256]{2,1,0:T(2,128)(2,1)S(1)}, bf16[128,2,256]{2,1,0:T(2,128)(2,1)}, u32[]{:S(2)}) copy-start(bf16[128,2,256]{2,1,0:T(2,128)(2,1)} %param.17) | copy-start | bytes 393220
  45.3 36.6 %all-to-all-start.1 = ((bf16[128,2,2304]{2,1,0:T(2,128)(2,1)}), bf16[128,2,2304]{2,1,0:T(2,128)(2,1)S(1)}, u32[]{:S(2)}, u32[]{:S(2)}) async-start(bf16[128,2,2304]{2,1,0:T(2,128)(2,1)} %reshape.42), calls=%async_computation.1 | async-start | bytes 2359296 | tf_op jit(solution)/shard_map/all_to_all | solution.py:394
  52.9 10.5 %collective-permute-start = (bf16[256,768]{1,0:T(8,128)(2,1)S(1)}, bf16[256,768]{1,0:T(8,128)(2,1)S(1)}, u32[]{:S(2)}, u32[]{:S(2)}) collective-permute-start(bf16[256,768]{1,0:T(8,128)(2,1)S(1)} %reshape.41.x), channel_id=1, source_target_pairs={{0,1},{1,0},{2,3},{3,2},{4,5},{5,4},{6,7},{7,6},{8,9},{9,8},{10,11... | collective-permute-start | bytes 1179656 | tf_op jit(solution)/shard_map/ppermute | solution.py:399
  63.4 0.8 copy-start.8
  72.8 9.6 %copy-start.4 = (f32[2,256]{1,0:T(2,128)S(1)}, f32[2,256]{1,0:T(2,128)}, u32[]{:S(2)}) copy-start(f32[2,256]{1,0:T(2,128)} %tower.9) | copy-start | bytes 6148
  72.8 9.6 %copy-start.5 = (f32[2]{0:T(128)S(1)}, f32[2]{0:T(128)}, u32[]{:S(2)}) copy-start(f32[2]{0:T(128)} %bias.1) | copy-start | bytes 28
  82.4 33.9 %copy-start.2 = (bf16[256,768]{1,0:T(8,128)(2,1)S(1)}, bf16[256,768]{1,0:T(8,128)(2,1)}, u32[]{:S(2)}) copy-start(bf16[256,768]{1,0:T(8,128)(2,1)} %copy-done.1) | copy-start | bytes 1179652
  82.4 33.9 %copy-start.7 = (f32[1024,256]{1,0:T(8,128)S(1)}, f32[1024,256]{1,0:T(8,128)}, u32[]{:S(2)}) copy-start(f32[1024,256]{1,0:T(8,128)} %table.1) | copy-start | bytes 3145732
  86.6 31.4 %copy-start = (f32[2048,128]{1,0:T(8,128)S(1)}, f32[2048,128]{1,0:T(8,128)}, u32[]{:S(2)}) copy-start(f32[2048,128]{1,0:T(8,128)} %get-tuple-element.32.after.slope) | copy-start | bytes 3145732
  86.6 31.4 %copy-start.9 = (bf16[256,768]{1,0:T(8,128)(2,1)S(1)}, bf16[256,768]{1,0:T(8,128)(2,1)}, u32[]{:S(2)}) copy-start(bf16[256,768]{1,0:T(8,128)(2,1)} %copy-done.8) | copy-start | bytes 1179652
  111.2 6.8 %collective-permute-start.1 = (bf16[1024,256]{1,0:T(8,128)(2,1)S(1)}, bf16[1024,256]{1,0:T(8,128)(2,1)S(1)}, u32[]{:S(2)}, u32[]{:S(2)}) collective-permute-start(bf16[1024,256]{1,0:T(8,128)(2,1)S(1)} %bitcast.10), channel_id=1, source_target_pairs={{0,1},{1,0},{2,3},{3,2},{4,5},{5,4},{6,7},{7,6},{8,9},{9,8},{10,11... | collective-permute-start | bytes 1572872 | tf_op jit(solution)/shard_map/ppermute | solution.py:399
